TPU v7x, 128 devices: a whole 4x4x4 slice. The times are simulated.
128 devices in a mesh: walk: 16 (over y_hi, z, core), band: 8 (over y_lo, x).
Axes of the slice: x: 4, y: 4 (y_hi: 2, y_lo: 2; y = y_hi * 2 + y_lo), z: 4, core: 2. Of those that a mesh axis runs over, the one named last changes fastest.
Arguments:
- positions: float32 [2, 49152], P(None, 'walk'), may hold values from 0 to 1
- coefficients: bfloat16 [2, 18432, 1024], P(None, 'walk', 'band')
- lattice: int32 [2, 18432], replicated, may hold values from -76 to 76
- spin_labels: int32 [49152], P('walk'), may hold values from 0 to 1
- occupied: int32 [2, 48], replicated, may hold values from 0 to 1023
- features: bfloat16 [49152, 256], P('walk'), may hold values from -6 to 6
- orbital_head: bfloat16 [256, 192], replicated, may hold values from -0.029907227 to 0.029907227
Outputs:
- gradient: float32 [256, 192], replicated
All inputs are finite; a program needn't handle non-finite values.
Results may differ from a plain program's by a relative error of at most 0.0003.
Values may be sent and summed in bfloat16 or wider, within the bound.
No kernel may reach another device: no remote copies, remote signals or barrier semaphores. Data moves between devices by JAX's collectives and lax.ppermute only.
A program may use at most 128 MiB of HBM per device.

v0:
```python
import jax
import jax.numpy as jnp
from jax import lax
from jax.sharding import PartitionSpec as P

E = 96


TWO_PI = 6.283185307179586


def orbital_block(pos_x, pos_y, lat_x, lat_y, right_cos, right_sin):
    phase_angle = TWO_PI * (pos_x[:, None] * lat_x[None, :] + pos_y[:, None] * lat_y[None, :])
    cosine = jnp.cos(phase_angle)
    sine_part = jnp.sin(phase_angle)
    first = jnp.dot(
        cosine, right_cos, precision=lax.Precision.HIGHEST, preferred_element_type=jnp.float32
    )
    second = jnp.dot(
        sine_part, right_sin, precision=lax.Precision.HIGHEST, preferred_element_type=jnp.float32
    )
    return first + second


def spin_columns(orbitals, spin_labels):
    orbital_count = orbitals.shape[1] // 4
    spin_up = (spin_labels == 0)[:, None]
    real_pick = jnp.where(
        spin_up, orbitals[:, :orbital_count], orbitals[:, orbital_count : 2 * orbital_count]
    )
    imag_pick = jnp.where(
        spin_up,
        orbitals[:, 2 * orbital_count : 3 * orbital_count],
        orbitals[:, 3 * orbital_count :],
    )
    return jnp.concatenate([real_pick, imag_pick], axis=1)


def fit_from_target(target, spin_labels, features, orbital_head, walkers):
    half_width = target.shape[1]
    spin_up = (spin_labels == 0)[:, None]
    net_all = jnp.dot(features, orbital_head, preferred_element_type=jnp.float32)
    net_value = jnp.where(spin_up, net_all[:, :half_width], net_all[:, half_width:])
    scaled = (net_value - target) / walkers
    blank_rows = jnp.zeros_like(scaled)
    spread_rows = jnp.concatenate(
        [jnp.where(spin_up, scaled, blank_rows), jnp.where(spin_up, blank_rows, scaled)], axis=1
    )
    return lax.dot_general(
        features.astype(jnp.float32),
        spread_rows,
        (((0,), (0,)), ((), ())),
        precision=lax.Precision.HIGHEST,
        preferred_element_type=jnp.float32,
    )


def fit_gradient(orbitals, spin_labels, features, orbital_head, walkers):
    target = spin_columns(orbitals, spin_labels)
    return fit_from_target(target, spin_labels, features, orbital_head, walkers)


def local(positions, coefficients, lattice, spin_labels, occupied, features, orbital_head):
    walk_count = lax.axis_size("walk")
    band_count = lax.axis_size("band")
    band_index = lax.axis_index("band")
    occ_flat = occupied.reshape(-1)
    wave_count = lattice.shape[1]
    gathered = lax.all_gather(coefficients, "walk", axis=1, tiled=True)
    band_panel = lax.all_to_all(gathered, "band", split_axis=1, concat_axis=2, tiled=True)
    picked = jnp.take(band_panel, occ_flat, axis=2)
    local_lattice = lax.dynamic_slice_in_dim(
        lattice, band_index * (wave_count // band_count), wave_count // band_count, 1
    )
    right_cos = jnp.concatenate([picked[0], picked[1]], axis=1).astype(jnp.float32)
    right_sin = jnp.concatenate([-picked[1], picked[0]], axis=1).astype(jnp.float32)
    lat_x = local_lattice[0].astype(jnp.float32)
    lat_y = local_lattice[1].astype(jnp.float32)
    local_count = positions.shape[1]
    block_rows = min(384, local_count)
    block_count = local_count // block_rows
    pos_x = positions[0].reshape(block_count, block_rows)
    pos_y = positions[1].reshape(block_count, block_rows)
    partial_value = lax.map(
        lambda coords: orbital_block(coords[0], coords[1], lat_x, lat_y, right_cos, right_sin),
        (pos_x, pos_y),
    )
    partial_value = partial_value.reshape(local_count, right_cos.shape[1])
    walkers = float(walk_count * local_count // E)
    orbitals = lax.psum(partial_value, "band")
    gradient = fit_gradient(orbitals, spin_labels, features, orbital_head, walkers)
    return lax.psum(gradient, "walk")


def solution(mesh):
    return jax.shard_map(
        local,
        mesh=mesh,
        in_specs=(
            P(None, "walk"),
            P(None, "walk", "band"),
            P(),
            P("walk"),
            P(),
            P("walk", None),
            P(),
        ),
        out_specs=P(),
        check_vma=False,
    )
```

profile of v0, /device:TPU:0, one launch (start us, length us, event | category | flops | bytes accessed | tf_op | source)
XLA Modules:
  0.0 891.4 jit_solution(2126646476932792642)
XLA Ops:
  12.7 79.9 %all-gather.2.cloned.1.call-done = bf16[2,18432,128]{2,0,1:T(2,128)(2,1)} async-done(((bf16[2,1152,128]{2,0,1:T(2,128)(2,1)}), bf16[2,18432,128]{2,0,1:T(2,128)(2,1)}) %all-gather.2.cloned.1.call-update) | async-done | bytes 9437200 | tf_op jit(solution)/shard_map/all_gather | solution.py:69
  98.9 105.0 %all-to-all-done = bf16[2,18432,128]{2,0,1:T(2,128)(2,1)} async-done(((bf16[2,18432,128]{2,0,1:T(2,128)(2,1)}), bf16[2,18432,128]{2,0,1:T(2,128)(2,1)}, u32[]{:S(2)}, u32[]{:S(2)}) %all-to-all-start) | async-done | bytes 9437216 | tf_op jit(solution)/shard_map/all_to_all | solution.py:70
  203.9 10.1 %copy.32 = bf16[2,18432,128]{2,1,0:T(8,128)(2,1)} copy(bf16[2,18432,128]{2,0,1:T(2,128)(2,1)} %all-to-all-done) | data formatting | bytes 18874368 | tf_op jit(solution)/shard_map/all_to_all | solution.py:70
  214.0 12.9 %copy.33 = bf16[2,2304,8,128]{1,3,2,0:T(8,128)(2,1)} copy(bf16[2,2304,8,128]{3,1,2,0:T(8,128)(2,1)} %bitcast.33) | data formatting | bytes 18874368 | tf_op jit(solution)/shard_map/all_to_all | solution.py:70
  226.9 18.4 %copy.34 = bf16[2,2304,1024]{1,0,2:T(2,128)(2,1)} copy(bf16[2,2304,1024]{1,2,0:T(8,128)(2,1)} %bitcast.34) | data formatting | bytes 18874368 | tf_op jit(solution)/shard_map/all_to_all | solution.py:70
  259.9 364.3 %while.10 = (s32[]{:T(128)}, f32[8,384,192]{1,0,2:T(8,128)}, f32[8,384]{1,0:T(8,128)S(1)}, f32[2304]{0:T(1024)S(1)}, f32[8,384]{1,0:T(8,128)S(1)}, /*index=5*/f3...) while((s32[]{:T(128)}, f32[8,384,192]{1,0,2:T(8,128)}, ...), condition=%wide.region_1.2_spmd, body=%wide.region_0.1_spmd.sunk | while | flops 4084015104 | bytes 12730505 | solution.py:84
  282.6 18.3 %fusion.54 = f32[384,192]{0,1:T(8,128)S(1)} fusion(f32[2304,192]{1,0:T(8,128)} %get-tuple-element.200, f32[2304]{0:T(1024)S(1)} %get-tuple-element.198, f32[384]{0:T(512)S(1)} %get-tuple-element.171, f32[2304]{0:T(1024)S(1)} %get-tuple-element.196, f32[384]{0:T(512)S(1)} %get-tuple-element.172), kind=kOutput, calls=%fused_computation.1.clone.1 | convolution fusion | flops 2041970688 | bytes 2085888 | tf_op jit(solution)/shard_map/while/body/eval_jaxpr/dot_general | solution.py:19
  300.9 16.4 %fusion.55 = f32[1,384,192]{1,2,0:T(8,128)S(1)} fusion(f32[384,192]{0,1:T(8,128)S(1)} %fusion.54, f32[2304,192]{1,0:T(8,128)S(1)} %copy-done.2, f32[2304]{0:T(1024)S(1)} %get-tuple-element.198, f32[384]{0:T(512)S(1)} %get-tuple-element.171, f32[2304]{0:T(1024)S(1)} %get-tuple-element.196, f32[384]{0:T(512)S(1)} %get-tuple-element.172), kind=kOutput, calls=%fused_computation.17.clone.1 | convolution fusion | flops 2042044416 | bytes 2380800 | tf_op jit(solution)/shard_map/while/body/eval_jaxpr/dot_general | solution.py:16
  317.7 7.3 dynamic_update_slice.5
  325.0 18.3 %fusion.54 = f32[384,192]{0,1:T(8,128)S(1)} fusion(f32[2304,192]{1,0:T(8,128)} %get-tuple-element.200, f32[2304]{0:T(1024)S(1)} %get-tuple-element.198, f32[384]{0:T(512)S(1)} %get-tuple-element.171, f32[2304]{0:T(1024)S(1)} %get-tuple-element.196, f32[384]{0:T(512)S(1)} %get-tuple-element.172), kind=kOutput, calls=%fused_computation.1.clone.1 | convolution fusion | flops 2041970688 | bytes 2085888 | tf_op jit(solution)/shard_map/while/body/eval_jaxpr/dot_general | solution.py:19
  343.3 16.4 %fusion.55 = f32[1,384,192]{1,2,0:T(8,128)S(1)} fusion(f32[384,192]{0,1:T(8,128)S(1)} %fusion.54, f32[2304,192]{1,0:T(8,128)S(1)} %copy-done.2, f32[2304]{0:T(1024)S(1)} %get-tuple-element.198, f32[384]{0:T(512)S(1)} %get-tuple-element.171, f32[2304]{0:T(1024)S(1)} %get-tuple-element.196, f32[384]{0:T(512)S(1)} %get-tuple-element.172), kind=kOutput, calls=%fused_computation.17.clone.1 | convolution fusion | flops 2042044416 | bytes 2380800 | tf_op jit(solution)/shard_map/while/body/eval_jaxpr/dot_general | solution.py:16
  360.0 7.3 dynamic_update_slice.5
  367.4 18.3 %fusion.54 = f32[384,192]{0,1:T(8,128)S(1)} fusion(f32[2304,192]{1,0:T(8,128)} %get-tuple-element.200, f32[2304]{0:T(1024)S(1)} %get-tuple-element.198, f32[384]{0:T(512)S(1)} %get-tuple-element.171, f32[2304]{0:T(1024)S(1)} %get-tuple-element.196, f32[384]{0:T(512)S(1)} %get-tuple-element.172), kind=kOutput, calls=%fused_computation.1.clone.1 | convolution fusion | flops 2041970688 | bytes 2085888 | tf_op jit(solution)/shard_map/while/body/eval_jaxpr/dot_general | solution.py:19
  385.7 16.4 %fusion.55 = f32[1,384,192]{1,2,0:T(8,128)S(1)} fusion(f32[384,192]{0,1:T(8,128)S(1)} %fusion.54, f32[2304,192]{1,0:T(8,128)S(1)} %copy-done.2, f32[2304]{0:T(1024)S(1)} %get-tuple-element.198, f32[384]{0:T(512)S(1)} %get-tuple-element.171, f32[2304]{0:T(1024)S(1)} %get-tuple-element.196, f32[384]{0:T(512)S(1)} %get-tuple-element.172), kind=kOutput, calls=%fused_computation.17.clone.1 | convolution fusion | flops 2042044416 | bytes 2380800 | tf_op jit(solution)/shard_map/while/body/eval_jaxpr/dot_general | solution.py:16
  402.4 7.3 dynamic_update_slice.5
  409.7 18.3 %fusion.54 = f32[384,192]{0,1:T(8,128)S(1)} fusion(f32[2304,192]{1,0:T(8,128)} %get-tuple-element.200, f32[2304]{0:T(1024)S(1)} %get-tuple-element.198, f32[384]{0:T(512)S(1)} %get-tuple-element.171, f32[2304]{0:T(1024)S(1)} %get-tuple-element.196, f32[384]{0:T(512)S(1)} %get-tuple-element.172), kind=kOutput, calls=%fused_computation.1.clone.1 | convolution fusion | flops 2041970688 | bytes 2085888 | tf_op jit(solution)/shard_map/while/body/eval_jaxpr/dot_general | solution.py:19
  428.1 16.4 %fusion.55 = f32[1,384,192]{1,2,0:T(8,128)S(1)} fusion(f32[384,192]{0,1:T(8,128)S(1)} %fusion.54, f32[2304,192]{1,0:T(8,128)S(1)} %copy-done.2, f32[2304]{0:T(1024)S(1)} %get-tuple-element.198, f32[384]{0:T(512)S(1)} %get-tuple-element.171, f32[2304]{0:T(1024)S(1)} %get-tuple-element.196, f32[384]{0:T(512)S(1)} %get-tuple-element.172), kind=kOutput, calls=%fused_computation.17.clone.1 | convolution fusion | flops 2042044416 | bytes 2380800 | tf_op jit(solution)/shard_map/while/body/eval_jaxpr/dot_general | solution.py:16
  444.8 7.3 dynamic_update_slice.5
  452.1 18.3 %fusion.54 = f32[384,192]{0,1:T(8,128)S(1)} fusion(f32[2304,192]{1,0:T(8,128)} %get-tuple-element.200, f32[2304]{0:T(1024)S(1)} %get-tuple-element.198, f32[384]{0:T(512)S(1)} %get-tuple-element.171, f32[2304]{0:T(1024)S(1)} %get-tuple-element.196, f32[384]{0:T(512)S(1)} %get-tuple-element.172), kind=kOutput, calls=%fused_computation.1.clone.1 | convolution fusion | flops 2041970688 | bytes 2085888 | tf_op jit(solution)/shard_map/while/body/eval_jaxpr/dot_general | solution.py:19
  470.4 16.4 %fusion.55 = f32[1,384,192]{1,2,0:T(8,128)S(1)} fusion(f32[384,192]{0,1:T(8,128)S(1)} %fusion.54, f32[2304,192]{1,0:T(8,128)S(1)} %copy-done.2, f32[2304]{0:T(1024)S(1)} %get-tuple-element.198, f32[384]{0:T(512)S(1)} %get-tuple-element.171, f32[2304]{0:T(1024)S(1)} %get-tuple-element.196, f32[384]{0:T(512)S(1)} %get-tuple-element.172), kind=kOutput, calls=%fused_computation.17.clone.1 | convolution fusion | flops 2042044416 | bytes 2380800 | tf_op jit(solution)/shard_map/while/body/eval_jaxpr/dot_general | solution.py:16
  487.2 7.3 dynamic_update_slice.5
  494.5 18.3 %fusion.54 = f32[384,192]{0,1:T(8,128)S(1)} fusion(f32[2304,192]{1,0:T(8,128)} %get-tuple-element.200, f32[2304]{0:T(1024)S(1)} %get-tuple-element.198, f32[384]{0:T(512)S(1)} %get-tuple-element.171, f32[2304]{0:T(1024)S(1)} %get-tuple-element.196, f32[384]{0:T(512)S(1)} %get-tuple-element.172), kind=kOutput, calls=%fused_computation.1.clone.1 | convolution fusion | flops 2041970688 | bytes 2085888 | tf_op jit(solution)/shard_map/while/body/eval_jaxpr/dot_general | solution.py:19
  512.8 16.4 %fusion.55 = f32[1,384,192]{1,2,0:T(8,128)S(1)} fusion(f32[384,192]{0,1:T(8,128)S(1)} %fusion.54, f32[2304,192]{1,0:T(8,128)S(1)} %copy-done.2, f32[2304]{0:T(1024)S(1)} %get-tuple-element.198, f32[384]{0:T(512)S(1)} %get-tuple-element.171, f32[2304]{0:T(1024)S(1)} %get-tuple-element.196, f32[384]{0:T(512)S(1)} %get-tuple-element.172), kind=kOutput, calls=%fused_computation.17.clone.1 | convolution fusion | flops 2042044416 | bytes 2380800 | tf_op jit(solution)/shard_map/while/body/eval_jaxpr/dot_general | solution.py:16
  529.5 7.3 dynamic_update_slice.5
  536.9 18.3 %fusion.54 = f32[384,192]{0,1:T(8,128)S(1)} fusion(f32[2304,192]{1,0:T(8,128)} %get-tuple-element.200, f32[2304]{0:T(1024)S(1)} %get-tuple-element.198, f32[384]{0:T(512)S(1)} %get-tuple-element.171, f32[2304]{0:T(1024)S(1)} %get-tuple-element.196, f32[384]{0:T(512)S(1)} %get-tuple-element.172), kind=kOutput, calls=%fused_computation.1.clone.1 | convolution fusion | flops 2041970688 | bytes 2085888 | tf_op jit(solution)/shard_map/while/body/eval_jaxpr/dot_general | solution.py:19
  555.2 16.4 %fusion.55 = f32[1,384,192]{1,2,0:T(8,128)S(1)} fusion(f32[384,192]{0,1:T(8,128)S(1)} %fusion.54, f32[2304,192]{1,0:T(8,128)S(1)} %copy-done.2, f32[2304]{0:T(1024)S(1)} %get-tuple-element.198, f32[384]{0:T(512)S(1)} %get-tuple-element.171, f32[2304]{0:T(1024)S(1)} %get-tuple-element.196, f32[384]{0:T(512)S(1)} %get-tuple-element.172), kind=kOutput, calls=%fused_computation.17.clone.1 | convolution fusion | flops 2042044416 | bytes 2380800 | tf_op jit(solution)/shard_map/while/body/eval_jaxpr/dot_general | solution.py:16
  571.9 7.3 dynamic_update_slice.5
  579.2 18.3 %fusion.54 = f32[384,192]{0,1:T(8,128)S(1)} fusion(f32[2304,192]{1,0:T(8,128)} %get-tuple-element.200, f32[2304]{0:T(1024)S(1)} %get-tuple-element.198, f32[384]{0:T(512)S(1)} %get-tuple-element.171, f32[2304]{0:T(1024)S(1)} %get-tuple-element.196, f32[384]{0:T(512)S(1)} %get-tuple-element.172), kind=kOutput, calls=%fused_computation.1.clone.1 | convolution fusion | flops 2041970688 | bytes 2085888 | tf_op jit(solution)/shard_map/while/body/eval_jaxpr/dot_general | solution.py:19
  597.6 16.4 %fusion.55 = f32[1,384,192]{1,2,0:T(8,128)S(1)} fusion(f32[384,192]{0,1:T(8,128)S(1)} %fusion.54, f32[2304,192]{1,0:T(8,128)S(1)} %copy-done.2, f32[2304]{0:T(1024)S(1)} %get-tuple-element.198, f32[384]{0:T(512)S(1)} %get-tuple-element.171, f32[2304]{0:T(1024)S(1)} %get-tuple-element.196, f32[384]{0:T(512)S(1)} %get-tuple-element.172), kind=kOutput, calls=%fused_computation.17.clone.1 | convolution fusion | flops 2042044416 | bytes 2380800 | tf_op jit(solution)/shard_map/while/body/eval_jaxpr/dot_general | solution.py:16
  614.3 7.3 dynamic_update_slice.5
  630.7 114.0 %all-reduce.3.cloned.1.call-done = f32[3072,192]{0,1:T(8,128)} async-done(((f32[3072,192]{0,1:T(8,128)}), f32[3072,192]{0,1:T(8,128)}) %all-reduce.3.cloned.1.call-update) | async-done | bytes 2359312 | tf_op jit(solution)/shard_map/psum | solution.py:90
  749.4 133.6 %all-reduce.5.cloned.1.call-done = f32[256,192]{0,1:T(8,128)} async-done(((f32[256,192]{0,1:T(8,128)}), f32[256,192]{0,1:T(8,128)}) %all-reduce.5.cloned.1.call-update) | async-done | bytes 196624 | tf_op jit(solution)/shard_map/psum | solution.py:92
  (77 shorter events, 42.4 us)
Async XLA Ops:
  6.5 621.9 %copy-start = (bf16[3072,256]{1,0:T(8,128)(2,1)S(1)}, bf16[3072,256]{1,0:T(8,128)(2,1)}, u32[]{:S(2)}) copy-start(bf16[3072,256]{1,0:T(8,128)(2,1)} %param.14) | copy-start | bytes 4718596
  6.5 86.0 %all-gather.2.cloned.1.call-start = ((), (), s32[]{:S(2)}) async-start(), calls=%async_computation.1 | async-start | bytes 10027008 | tf_op jit(solution)/shard_map/all_gather | solution.py:69
  12.6 85.0 %copy-start.6 = (s32[2,48]{1,0:T(2,128)S(1)}, s32[2,48]{1,0:T(2,128)}, u32[]{:S(2)}) copy-start(s32[2,48]{1,0:T(2,128)} %param.13) | copy-start | bytes 1156
  12.6 85.2 %copy-start.4 = (f32[2,3072]{1,0:T(2,128)S(1)}, f32[2,3072]{1,0:T(2,128)}, u32[]{:S(2)}) copy-start(f32[2,3072]{1,0:T(2,128)} %param.9) | copy-start | bytes 73732
  92.5 111.3 %all-to-all-start = ((bf16[2,18432,128]{2,0,1:T(2,128)(2,1)}), bf16[2,18432,128]{2,0,1:T(2,128)(2,1)}, u32[]{:S(2)}, u32[]{:S(2)}) async-start(bf16[2,18432,128]{2,0,1:T(2,128)(2,1)} %all-gather.2.cloned.1.call-done), calls=%async_computation | async-start | bytes 18874368 | tf_op jit(solution)/shard_map/all_to_all | solution.py:70
  97.6 647.1 %all-reduce.3.cloned.1.call-start = ((), (), s32[]{:S(2)}) async-start(), calls=%async_computation.2 | async-start | bytes 4718592 | tf_op jit(solution)/shard_map/psum | solution.py:90
  282.6 18.3 %copy-start.2 = (f32[2304,192]{1,0:T(8,128)S(1)}, f32[2304,192]{1,0:T(8,128)}, u32[]{:S(2)}) copy-start(f32[2304,192]{1,0:T(8,128)} %get-tuple-element.199) | copy-start | bytes 5308420 | tf_op jit(solution)/shard_map/while
  325.0 18.3 %copy-start.2 = (f32[2304,192]{1,0:T(8,128)S(1)}, f32[2304,192]{1,0:T(8,128)}, u32[]{:S(2)}) copy-start(f32[2304,192]{1,0:T(8,128)} %get-tuple-element.199) | copy-start | bytes 5308420 | tf_op jit(solution)/shard_map/while
  367.3 18.3 %copy-start.2 = (f32[2304,192]{1,0:T(8,128)S(1)}, f32[2304,192]{1,0:T(8,128)}, u32[]{:S(2)}) copy-start(f32[2304,192]{1,0:T(8,128)} %get-tuple-element.199) | copy-start | bytes 5308420 | tf_op jit(solution)/shard_map/while
  409.7 18.3 %copy-start.2 = (f32[2304,192]{1,0:T(8,128)S(1)}, f32[2304,192]{1,0:T(8,128)}, u32[]{:S(2)}) copy-start(f32[2304,192]{1,0:T(8,128)} %get-tuple-element.199) | copy-start | bytes 5308420 | tf_op jit(solution)/shard_map/while
  452.1 18.3 %copy-start.2 = (f32[2304,192]{1,0:T(8,128)S(1)}, f32[2304,192]{1,0:T(8,128)}, u32[]{:S(2)}) copy-start(f32[2304,192]{1,0:T(8,128)} %get-tuple-element.199) | copy-start | bytes 5308420 | tf_op jit(solution)/shard_map/while
  494.5 18.3 %copy-start.2 = (f32[2304,192]{1,0:T(8,128)S(1)}, f32[2304,192]{1,0:T(8,128)}, u32[]{:S(2)}) copy-start(f32[2304,192]{1,0:T(8,128)} %get-tuple-element.199) | copy-start | bytes 5308420 | tf_op jit(solution)/shard_map/while
  536.8 18.3 %copy-start.2 = (f32[2304,192]{1,0:T(8,128)S(1)}, f32[2304,192]{1,0:T(8,128)}, u32[]{:S(2)}) copy-start(f32[2304,192]{1,0:T(8,128)} %get-tuple-element.199) | copy-start | bytes 5308420 | tf_op jit(solution)/shard_map/while
  579.2 18.3 %copy-start.2 = (f32[2304,192]{1,0:T(8,128)S(1)}, f32[2304,192]{1,0:T(8,128)}, u32[]{:S(2)}) copy-start(f32[2304,192]{1,0:T(8,128)} %get-tuple-element.199) | copy-start | bytes 5308420 | tf_op jit(solution)/shard_map/while
  627.7 0.7 copy-start.5
  627.7 0.9 copy-start.3
  627.8 255.3 %all-reduce.5.cloned.1.call-start = ((), (), s32[]{:S(2)}) async-start(), calls=%async_computation.3 | async-start | bytes 393216 | tf_op jit(solution)/shard_map/psum | solution.py:92
  744.7 2.4 copy-start.1
Sparse Core Ops, SparseCore 0:
  12.7 79.7 all-gather.1
  627.9 116.7 all-reduce.2
  749.6 133.4 all-reduce.4
where the time goes:
time: 901 us; the launch traced here: 891 us
  waiting for transfers between devices  433 us (48%)
  matrix products  282 us (31%)
  local copies, waits for them, and re-layouts  127 us (14%)
  loops' own time  25.6 us (3%)
  between operations  13.4 us (1%)
    dot_general x8, matrix products, orbital_block(): jnp.dot(sine_part, right_sin, precision=lax.Precision.HIGHEST, preferred_...  146 us
    psum x1, waiting for transfers between devices, local(): return lax.psum(gradient, 'walk')  134 us
    dot_general x8, matrix products, orbital_block(): jnp.dot(cosine, right_cos, precision=lax.Precision.HIGHEST, preferred_ele...  131 us
    psum x1, waiting for transfers between devices, local(): orbitals = lax.psum(partial_value, 'band')  114 us
    all_to_all x1, waiting for transfers between devices, local(): lax.all_to_all(gathered, 'band', split_axis=1, concat_axis=2, tiled=True)  105 us
    all_gather x1, waiting for transfers between devices, local(): gathered = lax.all_gather(coefficients, 'walk', axis=1, tiled=True)  79.9 us
    dynamic_update_slice x16, local copies, waits for them, and re-layouts, local(): lax.map(lambda coords: orbital_block(coords[0], coords[1], lat_x, lat_y,...  60.7 us
    all_to_all x3, local copies, waits for them, and re-layouts, local(): lax.all_to_all(gathered, 'band', split_axis=1, concat_axis=2, tiled=True)  41.4 us
  transfers between devices with their start and end apart: 4, of which 4 were waited for; matrix products, arithmetic and copies ran while one was open for 0% of the time, Pallas kernels for 0%

commit v1 on v0

v1 whole, which is shorter than its diff:
```python
import functools

import jax
import jax.numpy as jnp
from jax import lax
from jax.experimental import pallas as pl
from jax.experimental.pallas import tpu as pltpu
from jax.sharding import PartitionSpec as P

INTERPRET = False
F32 = jnp.float32
BF16 = jnp.bfloat16
PI = 3.141592653589793
HALF = 80
LANES = 128


def split3(value):
    high = value.astype(BF16)
    rest = value - high.astype(F32)
    middle = rest.astype(BF16)
    low = (rest - middle.astype(F32)).astype(BF16)
    return high, middle, low


def send_kernel(coef_ref, pick_ref, pos_ref, out_ref):
    rows = coef_ref.shape[1]
    pick = pick_ref[...].astype(BF16)
    for part in range(2):
        taken = lax.dot_general(
            pick, coef_ref[part], (((1,), (1,)), ((), ())), preferred_element_type=F32
        )
        out_ref[:, part * rows : (part + 1) * rows] = taken.astype(BF16)
    pos = pos_ref[...]
    width = pos.shape[1]
    base = 2 * rows
    for index, piece in enumerate(split3(pos)):
        start = base + index * width
        out_ref[:, start : start + width] = jnp.broadcast_to(piece.astype(F32), (out_ref.shape[0], width)).astype(BF16)


def base_wave(turns):
    quarter = (turns - 0.5) * (0.5 * PI)
    square = quarter * quarter
    sine = quarter * (
        1.0 + square * (-1 / 6 + square * (1 / 120 + square * (-1 / 5040 + square * (1 / 362880))))
    )
    cosine = 1.0 + square * (
        -1 / 2 + square * (1 / 24 + square * (-1 / 720 + square * (1 / 40320 - square * (1 / 3628800))))
    )
    sine, cosine = 2.0 * sine * cosine, 1.0 - 2.0 * sine * sine
    sine, cosine = 2.0 * sine * cosine, 1.0 - 2.0 * sine * sine
    return -cosine, -sine


def times(left, right):
    return left[0] * right[0] - left[1] * right[1], left[1] * right[0] + left[0] * right[1]


def orbital_kernel(recv_ref, lat_ref, out_ref, sum_ref, table_ref, wave_ref, eight_ref, *, unroll):
    groups, senders, _ = recv_ref.shape
    rows = lat_ref.shape[2]
    base = 2 * rows
    piece = (recv_ref.shape[2] - base) // 6
    chunks = piece // LANES
    pairs = senders * chunks // 2

    sum_ref[...] = jnp.zeros_like(sum_ref)
    frequency = lax.broadcasted_iota(jnp.int32, (HALF, rows), 0)

    def fold(group, carry):
        both = jnp.sum(recv_ref[group, :, :base].astype(F32), axis=0, keepdims=True)
        c_real = both[:, :rows]
        c_imag = both[:, rows:]
        lat_a = lat_ref[0, pl.ds(group, 1), :]
        lat_b = lat_ref[1, pl.ds(group, 1), :]
        sign_a = jnp.where(lat_a < 0, -1.0, 1.0)
        sign_b = jnp.where(lat_b < 0, -1.0, 1.0)
        at_a = frequency == jnp.abs(lat_a)
        at_b = frequency == jnp.abs(lat_b)
        zero = jnp.zeros((), F32)
        left = jnp.concatenate(
            [
                jnp.where(at_a, value, zero).astype(BF16)
                for value in (c_real, c_real * sign_a, c_imag, c_imag * sign_a)
            ],
            axis=0,
        )
        right = jnp.concatenate(
            [jnp.where(at_b, value, zero).astype(BF16) for value in (jnp.ones_like(sign_b), sign_b)], axis=0
        )
        sum_ref[...] += lax.dot_general(left, right, (((1,), (1,)), ((), ())), preferred_element_type=F32)
        return carry

    lax.fori_loop(0, groups, fold, 0)
    real_even = sum_ref[0:HALF, :]
    real_odd = sum_ref[HALF : 2 * HALF, :]
    imag_even = sum_ref[2 * HALF : 3 * HALF, :]
    imag_odd = sum_ref[3 * HALF : 4 * HALF, :]
    even = lax.broadcasted_iota(jnp.int32, real_even.shape, 1) < HALF
    table = jnp.concatenate(
        [
            jnp.where(even, real_even, -imag_even),
            jnp.where(even, -imag_odd, -real_odd),
            jnp.where(even, imag_even, real_even),
            jnp.where(even, real_odd, -imag_odd),
        ],
        axis=0,
    )
    high = table.astype(BF16).astype(F32)
    low = table - high
    pad = jnp.zeros((4 * HALF, table_ref.shape[1] - 6 * HALF), F32)
    table_ref[...] = jnp.concatenate([high, high, low, pad], axis=1).astype(BF16)

    def waves(group, carry):
        for chunk in range(chunks):
            for axis in range(2):
                turns = jnp.zeros((senders, LANES), F32)
                for part in range(3):
                    start = base + (part * 2 + axis) * piece + chunk * LANES
                    turns = turns + recv_ref[group, :, start : start + LANES].astype(F32)
                first = base_wave(turns)
                power = (jnp.ones_like(turns), jnp.zeros_like(turns))
                for k in range(8):
                    for half in range(2):
                        wave_ref[2 * axis + half, group, pl.ds(chunk * 8 + k, senders, stride=chunks * 8), :] = power[half]
                    power = first if k == 0 else times(power, first)
                for half in range(2):
                    eight_ref[2 * axis + half, group, pl.ds(chunk, senders, stride=chunks), :] = power[half]
        return carry

    lax.fori_loop(0, groups, waves, 0)

    def basis(group, chunk, axis):
        cosines, sines = [], []
        now = tuple(wave_ref[2 * axis + half, group, pl.ds(chunk * 8, 8), :] for half in range(2))
        step = tuple(
            jnp.broadcast_to(eight_ref[2 * axis + half, group, pl.ds(chunk, 1), :], (8, LANES)) for half in range(2)
        )
        for block in range(HALF // 8):
            cosines.append(now[0])
            sines.append(now[1])
            if block < HALF // 8 - 1:
                now = times(now, step)
        return jnp.concatenate(cosines + sines, axis=0)

    zeros = jnp.zeros((table_ref.shape[1] - 6 * HALF, 2 * LANES), BF16)

    def evaluate(index, carry):
        for inner in range(unroll):
            flat = index * unroll + inner
            group = flat // pairs
            pair = flat % pairs
            wave_y = jnp.concatenate([basis(group, pair * 2 + side, 1) for side in range(2)], axis=1)
            high_y = wave_y.astype(BF16)
            low_y = (wave_y - high_y.astype(F32)).astype(BF16)
            weights = jnp.concatenate([high_y, low_y, high_y, zeros], axis=0)
            inside = jnp.dot(table_ref[...], weights, preferred_element_type=F32)
            wave_x = jnp.concatenate([basis(group, pair * 2 + side, 0) for side in range(2)], axis=1)
            for half in range(2):
                value = jnp.sum(inside[half * 2 * HALF : (half + 1) * 2 * HALF, :] * wave_x, axis=0, keepdims=True)
                start = pl.multiple_of(half * senders * piece + pair * 2 * LANES, 2 * LANES)
                out_ref[pl.ds(group, 1), pl.ds(start, 2 * LANES)] = value
        return carry

    lax.fori_loop(0, groups * pairs // unroll, evaluate, 0)


def gradient_kernel(target_ref, feature_ref, head_ref, mask_ref, out_ref, *, scale):
    count = feature_ref.shape[0]
    slots = target_ref.shape[0]
    features = feature_ref[...]
    net = lax.dot_general(head_ref[...], features, (((1,), (1,)), ((), ())), preferred_element_type=F32)
    mine = mask_ref[...] != 0
    parts = []
    for half in range(2):
        scaled = (net[half * slots : (half + 1) * slots, :] - target_ref[:, half * count : (half + 1) * count]) * scale
        parts.append(jnp.where(mine, scaled, 0.0))
    spread = jnp.concatenate(parts, axis=0)
    total = jnp.zeros(out_ref.shape, F32)
    for piece in split3(spread):
        total = total + jnp.dot(piece, features, preferred_element_type=F32)
    out_ref[...] = total


def call(kernel, out, scratch=(), name=None):
    return pl.pallas_call(
        kernel,
        out_shape=out,
        scratch_shapes=list(scratch),
        name=name,
        interpret=INTERPRET,
        compiler_params=pltpu.CompilerParams(vmem_limit_bytes=48 * 1024 * 1024),
    )


def local(positions, coefficients, lattice, spin_labels, occupied, features, orbital_head):
    walk_count = lax.axis_size("walk")
    band_count = lax.axis_size("band")
    everyone = ("walk", "band")
    devices = walk_count * band_count
    band_index = lax.axis_index("band")
    rows = coefficients.shape[1]
    bands = coefficients.shape[2]
    count = positions.shape[1]
    piece = count // band_count
    orbitals = occupied.shape[0] * occupied.shape[1]
    each = orbitals // band_count

    by_device = jnp.transpose(occupied.reshape(band_count, each).astype(jnp.int32))
    by_device = jnp.concatenate([by_device, jnp.full((walk_count - each, band_count), -1, jnp.int32)], axis=0)
    wanted = by_device.reshape(devices, 1) - band_index * bands
    pick = (wanted == lax.broadcasted_iota(jnp.int32, (devices, bands), 1)).astype(F32)
    share = lax.dynamic_slice_in_dim(positions, band_index * piece, piece, 1).reshape(1, 2 * piece)
    sent = call(
        send_kernel, jax.ShapeDtypeStruct((devices, 2 * rows + 6 * piece), BF16), name="send"
    )(coefficients, pick, share)
    received = lax.all_to_all(sent, everyone, 0, 0, tiled=True)
    received = received.reshape(walk_count, band_count, sent.shape[1])

    chunks = count // LANES
    values = call(
        functools.partial(orbital_kernel, unroll=4),
        jax.ShapeDtypeStruct((walk_count, 2 * count), F32),
        [
            pltpu.VMEM((4 * HALF, 2 * HALF), F32),
            pltpu.VMEM((4 * HALF, 512), BF16),
            pltpu.VMEM((4, walk_count, 8 * chunks, LANES), F32),
            pltpu.VMEM((4, walk_count, chunks, LANES), F32),
        ],
        name="orbital",
    )(received, lattice.reshape(2, walk_count, rows))
    target = lax.all_to_all(values, "walk", 0, 0, tiled=True)

    spins = occupied.shape[0]
    per_spin = band_count // spins
    spin = band_index // per_spin
    columns = orbital_head.reshape(orbital_head.shape[0], spins, 2, per_spin, each)
    columns = lax.dynamic_index_in_dim(columns, spin, 1, keepdims=False)
    columns = lax.dynamic_index_in_dim(columns, band_index % per_spin, 2, keepdims=False)
    columns = jnp.transpose(columns, (1, 2, 0))
    columns = jnp.pad(columns, ((0, 0), (0, walk_count - each), (0, 0))).reshape(2 * walk_count, -1)
    mine = (spin_labels == spin).astype(jnp.int32).reshape(1, count)
    walkers = walk_count * count // orbitals
    hidden = features.shape[1]
    own = call(
        functools.partial(gradient_kernel, scale=1.0 / walkers),
        jax.ShapeDtypeStruct((2 * walk_count, hidden), F32),
        name="gradient",
    )(target, features, columns, mine)
    own = own.reshape(2, walk_count, hidden)[:, :each].reshape(-1, LANES)
    shares = lax.all_to_all(jnp.broadcast_to(own, (walk_count, *own.shape)), "walk", 0, 0, tiled=True)
    summed = jnp.sum(shares, axis=0)
    whole = lax.all_to_all(jnp.broadcast_to(summed, (band_count, *own.shape)), "band", 0, 0, tiled=True)
    whole = whole.reshape(spins, per_spin, 2, each, hidden)
    return jnp.transpose(whole, (4, 0, 2, 1, 3)).reshape(hidden, 2 * orbitals)


def solution(mesh):
    return jax.shard_map(
        local,
        mesh=mesh,
        in_specs=(
            P(None, "walk"),
            P(None, "walk", "band"),
            P(),
            P("walk"),
            P(),
            P("walk", None),
            P(),
        ),
        out_specs=P(),
        check_vma=False,
    )
```

time: 901 us -> 122 us (0.14)
  waiting for transfers between devices: 433 us -> 30.6 us
  matrix products: 282 us -> 0 us
  local copies, waits for them, and re-layouts: 127 us -> 12.8 us
  Pallas kernels: 0 us -> 37.6 us
  loops' own time: 25.6 us -> 0 us
  blocking collectives: 0 us -> 22.9 us
  between operations: 13.4 us -> 0.28 us
  starting transfers between devices: 5.13 us -> 15.2 us
    dot_general x18 -> x0, matrix products: 282 us -> none  [the longest x8 146 us: orbital_block(): jnp.dot(sine_part, right_sin, precision=lax.Precision.HIGHEST, preferred_...]
    psum x2 -> x0, waiting for transfers between devices: 248 us -> none  [the longest x1 134 us: local(): return lax.psum(gradient, 'walk')]
    all_gather x1 -> x0, waiting for transfers between devices: 79.9 us -> none  [local(): gathered = lax.all_gather(coefficients, 'walk', axis=1, tiled=True)]
    all_to_all x1 -> x2, waiting for transfers between devices: 105 us -> 30.6 us  [the longest x1 19.8 us: local(): received = lax.all_to_all(sent, everyone, 0, 0, tiled=True)]
    dynamic_update_slice x16 -> x0, local copies, waits for them, and re-layouts: 60.7 us -> none  [local(): lax.map(lambda coords: orbital_block(coords[0], coords[1], lat_x, lat_y,...]
    all_to_all x3 -> x2, local copies, waits for them, and re-layouts: 41.4 us -> 1.67 us  [the longest x1 1.15 us: local(): target = lax.all_to_all(values, 'walk', 0, 0, tiled=True)]
    pallas_call x0 -> x3, Pallas kernels: none -> 37.6 us  [the longest x1 35.4 us: local(): call(functools.partial(orbital_kernel, unroll=4), jax.ShapeDtypeStruct((w...]
    another operation x1 -> x0, loops' own time: 25.6 us -> none  [local(): lax.map(lambda coords: orbital_block(coords[0], coords[1], lat_x, lat_y,...]
  transfers between devices with their start and end apart: 4 -> 2, of which waited for: 4 -> 2; matrix products, arithmetic and copies ran while one was open for 0% -> 0% of each run, Pallas kernels for 0% -> 0%
where the time goes in v1:
time: 122 us; the launch traced here: 121 us
  Pallas kernels  37.6 us (31%)
  waiting for transfers between devices  30.6 us (25%)
  blocking collectives  22.9 us (19%)
  starting transfers between devices  15.2 us (12%)
  local copies, waits for them, and re-layouts  12.8 us (10%)
  other arithmetic  1.64 us (1%)
    pallas_call x1, Pallas kernels, local(): call(functools.partial(orbital_kernel, unroll=4), jax.ShapeDtypeStruct((w...  35.4 us
    all_to_all x1, waiting for transfers between devices, local(): received = lax.all_to_all(sent, everyone, 0, 0, tiled=True)  19.8 us
    all_to_all x1, blocking collectives, local(): lax.all_to_all(jnp.broadcast_to(own, (walk_count, *own.shape)), 'walk', 0...  13.5 us
    all_to_all x1, starting transfers between devices, local(): received = lax.all_to_all(sent, everyone, 0, 0, tiled=True)  11.6 us
    all_to_all x1, waiting for transfers between devices, local(): target = lax.all_to_all(values, 'walk', 0, 0, tiled=True)  10.8 us
    unnamed x19, local copies, waits for them, and re-layouts  9.35 us
    all_to_all x1, blocking collectives, local(): lax.all_to_all(jnp.broadcast_to(summed, (band_count, *own.shape)), 'band'...  9.34 us
    all_to_all x1, starting transfers between devices, local(): target = lax.all_to_all(values, 'walk', 0, 0, tiled=True)  3.55 us
  transfers between devices with their start and end apart: 2, of which 2 were waited for; matrix products, arithmetic and copies ran while one was open for 0% of the time, Pallas kernels for 0%

profile of v1, /device:TPU:0, one launch (start us, length us, event | category | flops | bytes accessed | tf_op | source)
XLA Modules:
  0.0 121.0 jit_solution(2726246371543116448)
XLA Ops:
  0.0 0.0 copy-start
  0.0 0.8 reshape.52
  0.8 0.1 copy.19
  0.8 0.1 sub.20
  0.9 0.1 fusion.pick_ref
  1.0 0.0 copy-done
  1.1 0.0 copy-start.2
  1.1 1.1 copy-done.2
  2.1 0.3 send.1
  2.5 0.5 broadcast.13
  3.0 1.5 %reduce = bf16[128,4608]{1,0:T(8,128)(2,1)S(1)} reduce(bf16[128,1,4608]{2,0,1:T(8,128)(2,1)S(1)} %bitcast.31, bf16[]{:T(256)} %broadcast.13), dimensions={1}, to_apply=%copy.20.reduce_sub_computation | reduce | bytes 2359298 | tf_op jit(solution)/shard_map/all_to_all | solution.py:218
  4.5 1.2 reshape.67
  5.7 11.6 %all-to-all-start = ((bf16[128,2,2304]{2,1,0:T(2,128)(2,1)}), bf16[128,2,2304]{2,1,0:T(2,128)(2,1)}, u32[]{:S(2)}, u32[]{:S(2)}) async-start(bf16[128,2,2304]{2,1,0:T(2,128)(2,1)} %reshape.67), calls=%async_computation | async-start | bytes 2359296 | tf_op jit(solution)/shard_map/all_to_all | solution.py:218
  17.4 0.0 copy-done.3
  17.4 19.8 %all-to-all-done = bf16[128,2,2304]{2,1,0:T(2,128)(2,1)} async-done(((bf16[128,2,2304]{2,1,0:T(2,128)(2,1)}), bf16[128,2,2304]{2,1,0:T(2,128)(2,1)}, u32[]{:S(2)}, u32[]{:S(2)}) %all-to-all-start) | async-done | bytes 1179680 | tf_op jit(solution)/shard_map/all_to_all | solution.py:218
  37.2 6.8 %reshape.68 = bf16[128,1,4608]{2,1,0:T(2,128)(2,1)S(1)} reshape(bf16[128,2,2304]{2,1,0:T(2,128)(2,1)} %all-to-all-done) | data formatting | bytes 2359296
  44.0 0.2 copy.30
  44.1 35.4 %orbital.1 = f32[16,6144]{1,0:T(8,128)S(1)} custom-call(bf16[16,8,4608]{2,1,0:T(8,128)(2,1)S(1)} %bitcast.30, s32[2,16,1152]{2,1,0:T(8,128)S(1)} %bitcast.34), custom_call_target="tpu_custom_call" | custom-call | tf_op jit(solution)/shard_map/orbital/pallas_call | solution.py:222
  79.5 0.0 copy-start.4
  79.5 0.0 copy-start.5
  79.6 0.0 copy-start.1
  79.6 1.2 copy.21
  80.7 3.6 %all-to-all-start.1 = ((f32[16,1,6144]{2,1,0:T(1,128)}), f32[16,1,6144]{2,1,0:T(1,128)S(1)}, u32[]{:S(2)}, u32[]{:S(2)}) async-start(f32[16,1,6144]{2,1,0:T(1,128)} %copy.21), calls=%async_computation.1 | async-start | bytes 786432 | tf_op jit(solution)/shard_map/all_to_all | solution.py:233
  84.3 0.0 copy-done.4
  84.4 10.8 %all-to-all-done.1 = f32[16,1,6144]{2,1,0:T(1,128)S(1)} async-done(((f32[16,1,6144]{2,1,0:T(1,128)}), f32[16,1,6144]{2,1,0:T(1,128)S(1)}, u32[]{:S(2)}, u32[]{:S(2)}) %all-to-all-start.1) | async-done | bytes 393248 | tf_op jit(solution)/shard_map/all_to_all | solution.py:233
  95.2 0.1 copy.31
  95.3 0.0 copy-done.1
  95.3 1.9 %gradient.1 = f32[32,256]{1,0:T(8,128)S(1)} custom-call(f32[16,6144]{1,0:T(8,128)S(1)} %bitcast.33, bf16[3072,256]{1,0:T(8,128)(2,1)S(1)} %copy-done.1, bf16[32,256]{1,0:T(8,128)(2,1)S(1)} %bitcast.36, s32[1,3072]{1,0:T(1,128)S(1)} %bitcast.37), custom_call_target="tpu_custom_call" | custom-call | tf_op jit(solution)/shard_map/gradient/pallas_call | solution.py:246
  97.2 13.5 %all_to_all.30 = f32[16,48,128]{2,1,0:T(8,128)S(1)} all-to-all(f32[16,48,128]{2,1,0:T(8,128)S(1)} %broadcast_in_dim.7), channel_id=1, replica_groups=mesh['walk'=16,'band'=8] {'walk'}, dimensions={0} | all-to-all | bytes 786432 | tf_op jit(solution)/shard_map/all_to_all | solution.py:252
  110.8 9.3 %all_to_all.31 = f32[8,48,128]{2,1,0:T(8,128)S(1)} all-to-all(f32[8,48,128]{2,1,0:T(8,128)S(1)} %broadcast_in_dim.8), channel_id=1, replica_groups=mesh['walk'=16,'band'=8] {'band'}, dimensions={0} | all-to-all | bytes 393216 | tf_op jit(solution)/shard_map/all_to_all | solution.py:254
  120.2 0.1 reshape.62
  120.3 0.7 reshape.63
  (15 shorter events, 0.2 us)
Async XLA Ops:
  0.0 1.0 copy-start
  1.1 1.1 copy-start.2
  5.7 11.7 %copy-start.3 = (s32[2,18432]{1,0:T(2,128)S(1)}, s32[2,18432]{1,0:T(2,128)}, u32[]{:S(2)}) copy-start(s32[2,18432]{1,0:T(2,128)} %param.9) | copy-start | bytes 442372
  5.7 31.5 %all-to-all-start = ((bf16[128,2,2304]{2,1,0:T(2,128)(2,1)}), bf16[128,2,2304]{2,1,0:T(2,128)(2,1)}, u32[]{:S(2)}, u32[]{:S(2)}) async-start(bf16[128,2,2304]{2,1,0:T(2,128)(2,1)} %reshape.67), calls=%async_computation | async-start | bytes 2359296 | tf_op jit(solution)/shard_map/all_to_all | solution.py:218
  79.5 4.8 %copy-start.4 = (bf16[256,192]{0,1:T(8,128)(2,1)S(1)}, bf16[256,192]{0,1:T(8,128)(2,1)}, u32[]{:S(2)}) copy-start(bf16[256,192]{0,1:T(8,128)(2,1)} %param.13) | copy-start | bytes 294916
  79.5 4.9 %copy-start.5 = (s32[3072]{0:T(1024)S(1)}, s32[3072]{0:T(1024)}, u32[]{:S(2)}) copy-start(s32[3072]{0:T(1024)} %param.10) | copy-start | bytes 36868
  79.6 15.7 %copy-start.1 = (bf16[3072,256]{1,0:T(8,128)(2,1)S(1)}, bf16[3072,256]{1,0:T(8,128)(2,1)}, u32[]{:S(2)}) copy-start(bf16[3072,256]{1,0:T(8,128)(2,1)} %feature_ref.1) | copy-start | bytes 4718596
  80.7 14.5 %all-to-all-start.1 = ((f32[16,1,6144]{2,1,0:T(1,128)}), f32[16,1,6144]{2,1,0:T(1,128)S(1)}, u32[]{:S(2)}, u32[]{:S(2)}) async-start(f32[16,1,6144]{2,1,0:T(1,128)} %copy.21), calls=%async_computation.1 | async-start | bytes 786432 | tf_op jit(solution)/shard_map/all_to_all | solution.py:233

commit v2 on v1

v2 whole, which is shorter than its diff:
```python
import functools

import jax
import jax.numpy as jnp
from jax import lax
from jax.experimental import pallas as pl
from jax.experimental.pallas import tpu as pltpu
from jax.sharding import PartitionSpec as P

INTERPRET = False
F32 = jnp.float32
BF16 = jnp.bfloat16
PI = 3.141592653589793
BLOCK = 40
HALF = 80
LANES = 128


def split3(value):
    high = value.astype(BF16)
    rest = value - high.astype(F32)
    middle = rest.astype(BF16)
    low = (rest - middle.astype(F32)).astype(BF16)
    return high, middle, low


def coefficient_row(index):
    return 8 * (index // 2) + 6 + index % 2 if index < 6 else 18 + index


def send_kernel(coef_ref, occ_ref, pos_ref, label_ref, out_ref, slot_ref, stage_ref):
    rows = coef_ref.shape[1]
    bands = coef_ref.shape[2]
    devices = out_ref.shape[0] // BLOCK
    spins, per_spin = occ_ref.shape
    senders = lax.axis_size("band")
    each = spins * per_spin // senders
    count = pos_ref.shape[1]
    piece = count // senders
    tiles = rows // LANES
    mine = lax.axis_index("band")

    line = lax.broadcasted_iota(jnp.int32, (8, bands), 0)
    picks = []
    for group in range(devices // senders):
        if group >= each:
            picks.append(jnp.zeros((8, bands), F32))
            continue
        wanted = jnp.full((8, bands), -1, jnp.int32)
        for sender in range(senders):
            orbital = sender * each + group
            wanted = jnp.where(line == sender, occ_ref[orbital // per_spin, orbital % per_spin], wanted)
        lane = lax.broadcasted_iota(jnp.int32, (8, bands), 1) + mine * bands
        picks.append(jnp.where(lane == wanted, 1.0, 0.0))
    pick = jnp.concatenate(picks, axis=0).astype(BF16)
    for part in range(2):
        taken = lax.dot_general(
            pick, coef_ref[part], (((1,), (1,)), ((), ())), preferred_element_type=F32
        )
        for tile in range(tiles):
            at = coefficient_row(part * tiles + tile)
            stage_ref[pl.ds(at, devices, stride=BLOCK), :] = taken[:, tile * LANES : (tile + 1) * LANES]

    chunks = count // LANES
    up = label_ref[...] == 0
    ones = jnp.where(up, 1.0, 0.0)
    row = lax.broadcasted_iota(jnp.int32, (LANES, LANES), 0)
    column = lax.broadcasted_iota(jnp.int32, (LANES, LANES), 1)
    until = jnp.where(row <= column, 1.0, 0.0).astype(BF16)
    inside = jnp.dot(ones.astype(BF16), until, preferred_element_type=F32)
    whole = jnp.broadcast_to(inside[:, LANES - 1 : LANES], inside.shape)
    row = lax.broadcasted_iota(jnp.int32, (chunks, chunks), 0)
    column = lax.broadcasted_iota(jnp.int32, (chunks, chunks), 1)
    before = jnp.where(column < row, 1.0, 0.0).astype(BF16)
    rank = inside + jnp.dot(before, whole.astype(BF16), preferred_element_type=F32)
    total = jnp.sum(whole, axis=0, keepdims=True)
    place = (
        lax.broadcasted_iota(jnp.int32, rank.shape, 0) * LANES + lax.broadcasted_iota(jnp.int32, rank.shape, 1)
    ).astype(F32)
    slot = jnp.where(up, rank - 1.0, total + place - rank)
    slot = jnp.concatenate([slot[chunk : chunk + 1, :] for chunk in range(chunks)], axis=1)
    slot_ref[...] = slot
    here = lax.broadcasted_iota(jnp.int32, (piece, count), 0) + mine * piece
    move = jnp.where(here.astype(F32) == slot, 1.0, 0.0).astype(BF16)
    parts = jnp.concatenate([part.astype(F32) for part in split3(pos_ref[...])], axis=0).astype(BF16)
    moved = lax.dot_general(parts, move, (((1,), (1,)), ((), ())), preferred_element_type=F32)

    def everywhere(at, value):
        stage_ref[pl.ds(at, devices, stride=BLOCK), :] = jnp.broadcast_to(value, (devices, LANES))

    for part in range(3):
        for axis in range(2):
            for chunk in range(piece // LANES):
                at = 8 * part + axis * (piece // LANES) + chunk
                everywhere(at, moved[part * 2 + axis : part * 2 + axis + 1, chunk * LANES : (chunk + 1) * LANES])
    tens = jnp.floor(total * (1 / 64))
    everywhere(36, tens)
    everywhere(37, total - tens * 64.0)
    everywhere(38, jnp.zeros_like(total))
    everywhere(39, jnp.zeros_like(total))
    out_ref[...] = stage_ref[...].astype(BF16)


def sort_kernel(slot_ref, feature_ref, out_ref):
    count = feature_ref.shape[0]
    step = 384

    def block(index, carry):
        start = pl.multiple_of(index * step, step)
        here = lax.broadcasted_iota(jnp.int32, (step, count), 0) + start
        move = jnp.where(here.astype(F32) == slot_ref[...], 1.0, 0.0).astype(BF16)
        moved = jnp.dot(move, feature_ref[...], preferred_element_type=F32)
        out_ref[pl.ds(start, step), :] = moved.astype(BF16)
        return carry

    lax.fori_loop(0, count // step, block, 0)


def base_wave(turns):
    quarter = (turns - 0.5) * (0.5 * PI)
    square = quarter * quarter
    sine = quarter * (
        1.0 + square * (-1 / 6 + square * (1 / 120 + square * (-1 / 5040 + square * (1 / 362880))))
    )
    cosine = 1.0 + square * (
        -1 / 2 + square * (1 / 24 + square * (-1 / 720 + square * (1 / 40320 - square * (1 / 3628800))))
    )
    sine, cosine = 2.0 * sine * cosine, 1.0 - 2.0 * sine * sine
    sine, cosine = 2.0 * sine * cosine, 1.0 - 2.0 * sine * sine
    return -cosine, -sine


def times(left, right):
    return left[0] * right[0] - left[1] * right[1], left[1] * right[0] + left[0] * right[1]


def orbital_kernel(recv_ref, lat_ref, out_ref, sum_ref, table_ref, wave_ref, eight_ref, list_ref, *, unroll, each):
    groups = out_ref.shape[0]
    senders = recv_ref.shape[0] // groups
    rows = lat_ref.shape[2]
    tiles = rows // LANES
    chunks = out_ref.shape[1] // 2
    pairs = chunks // 2
    own = chunks // senders
    upper = lax.axis_index("band") < senders // 2
    active = lax.axis_index("walk") < each

    out_ref[...] = jnp.zeros_like(out_ref)
    sum_ref[...] = jnp.zeros_like(sum_ref)
    frequency = lax.broadcasted_iota(jnp.int32, (HALF, rows), 0)

    def fold(group, carry):
        both = jnp.zeros((BLOCK, LANES), F32)
        for sender in range(senders):
            both = both + recv_ref[group * senders + sender].astype(F32)
        c_real, c_imag = (
            jnp.concatenate([both[coefficient_row(k + t) :, :][:1] for t in range(tiles)], axis=1) for k in (0, tiles)
        )
        lat_a = lat_ref[0, pl.ds(group, 1), :]
        lat_b = lat_ref[1, pl.ds(group, 1), :]
        sign_a = jnp.where(lat_a < 0, -1.0, 1.0)
        sign_b = jnp.where(lat_b < 0, -1.0, 1.0)
        at_a = frequency == jnp.abs(lat_a)
        at_b = frequency == jnp.abs(lat_b)
        zero = jnp.zeros((), F32)
        left = jnp.concatenate(
            [
                jnp.where(at_a, value, zero).astype(BF16)
                for value in (c_real, c_real * sign_a, c_imag, c_imag * sign_a)
            ],
            axis=0,
        )
        right = jnp.concatenate(
            [jnp.where(at_b, value, zero).astype(BF16) for value in (jnp.ones_like(sign_b), sign_b)], axis=0
        )
        sum_ref[...] += lax.dot_general(left, right, (((1,), (1,)), ((), ())), preferred_element_type=F32)
        return carry

    lax.fori_loop(0, groups, fold, 0)
    real_even = sum_ref[0:HALF, :]
    real_odd = sum_ref[HALF : 2 * HALF, :]
    imag_even = sum_ref[2 * HALF : 3 * HALF, :]
    imag_odd = sum_ref[3 * HALF : 4 * HALF, :]
    even = lax.broadcasted_iota(jnp.int32, real_even.shape, 1) < HALF
    table = jnp.concatenate(
        [
            jnp.where(even, real_even, -imag_even),
            jnp.where(even, -imag_odd, -real_odd),
            jnp.where(even, imag_even, real_even),
            jnp.where(even, real_odd, -imag_odd),
        ],
        axis=0,
    )
    high = table.astype(BF16).astype(F32)
    low = table - high
    pad = jnp.zeros((4 * HALF, table_ref.shape[1] - 6 * HALF), F32)
    table_ref[...] = jnp.concatenate([high, high, low, pad], axis=1).astype(BF16)

    def waves(group, length):
        for sender in range(senders):
            block = recv_ref[group * senders + sender].astype(F32)
            first = base_wave(block[0:8] + block[8:16] + block[16:24])
            power = (jnp.ones((8, LANES), F32), jnp.zeros((8, LANES), F32))
            for k in range(8):
                for half in range(2):
                    wave_ref[half, group * senders + sender, pl.ds(k, 8, stride=8), :] = power[half]
                power = first if k == 0 else times(power, first)
            for half in range(2):
                eight_ref[half, group * senders + sender, :, :] = power[half]
            if sender == 0:
                number = (block[36:37, :] * 64.0 + block[37:38, :]).astype(jnp.int32)
        number = number[0, 0]
        low = jnp.where(upper, 0, number // (2 * LANES))
        high = jnp.where(upper, (number + 2 * LANES - 1) // (2 * LANES), pairs)
        high = jnp.where(active, high, low)

        def note(pair, at):
            list_ref[at] = group * pairs + pair
            return at + 1

        return lax.fori_loop(low, high, note, length)

    length = lax.fori_loop(0, groups, waves, 0)

    def basis(flat, axis):
        sender = flat // own
        line = axis * own + flat % own
        cosines, sines = [], []
        start = pl.multiple_of(line * 8, 8)
        now = tuple(wave_ref[half, sender, pl.ds(start, 8), :] for half in range(2))
        step = tuple(jnp.broadcast_to(eight_ref[half, sender, pl.ds(line, 1), :], (8, LANES)) for half in range(2))
        for block in range(HALF // 8):
            cosines.append(now[0])
            sines.append(now[1])
            if block < HALF // 8 - 1:
                now = times(now, step)
        return jnp.concatenate(cosines + sines, axis=0)

    zeros = jnp.zeros((table_ref.shape[1] - 6 * HALF, 2 * LANES), BF16)

    def evaluate(index, carry):
        for inner in range(unroll):
            entry = list_ref[jnp.minimum(index * unroll + inner, length - 1)]
            group = entry // pairs
            wave_y = jnp.concatenate([basis(entry * 2 + side, 1) for side in range(2)], axis=1)
            high_y = wave_y.astype(BF16)
            low_y = (wave_y - high_y.astype(F32)).astype(BF16)
            weights = jnp.concatenate([high_y, low_y, high_y, zeros], axis=0)
            inside = jnp.dot(table_ref[...], weights, preferred_element_type=F32)
            wave_x = jnp.concatenate([basis(entry * 2 + side, 0) for side in range(2)], axis=1)
            for half in range(2):
                value = jnp.sum(inside[half * 2 * HALF : (half + 1) * 2 * HALF, :] * wave_x, axis=0, keepdims=True)
                for side in range(2):
                    at = half * chunks + (entry - group * pairs) * 2 + side
                    out_ref[group, pl.ds(at, 1), :] = value[:, side * LANES : (side + 1) * LANES]
        return carry

    lax.fori_loop(0, (length + unroll - 1) // unroll, evaluate, 0)


def gradient_kernel(target_ref, feature_ref, head_ref, mask_ref, out_ref, *, scale):
    count = feature_ref.shape[0]
    chunks = count // LANES
    slots = head_ref.shape[0] // 2
    features = feature_ref[...]
    net = lax.dot_general(head_ref[...], features, (((1,), (1,)), ((), ())), preferred_element_type=F32)
    mine = mask_ref[...] != 0
    parts = []
    for half in range(2):
        target = jnp.concatenate(
            [target_ref[pl.ds(half * chunks + chunk, slots, stride=2 * chunks), :] for chunk in range(chunks)], axis=1
        )
        scaled = (net[half * slots : (half + 1) * slots, :] - target) * scale
        parts.append(jnp.where(mine, scaled, 0.0))
    spread = jnp.concatenate(parts, axis=0)
    total = jnp.zeros(out_ref.shape, F32)
    for piece in split3(spread):
        total = total + jnp.dot(piece, features, preferred_element_type=F32)
    out_ref[...] = total


def call(kernel, out, scratch=(), name=None, **more):
    return pl.pallas_call(
        kernel,
        out_shape=out,
        **more,
        scratch_shapes=list(scratch),
        name=name,
        interpret=INTERPRET,
        compiler_params=pltpu.CompilerParams(vmem_limit_bytes=48 * 1024 * 1024),
    )


def local(positions, coefficients, lattice, spin_labels, occupied, features, orbital_head):
    walk_count = lax.axis_size("walk")
    band_count = lax.axis_size("band")
    everyone = ("walk", "band")
    devices = walk_count * band_count
    band_index = lax.axis_index("band")
    rows = coefficients.shape[1]
    count = positions.shape[1]
    orbitals = occupied.shape[0] * occupied.shape[1]
    each = orbitals // band_count

    whole = pl.BlockSpec(memory_space=pltpu.VMEM)
    sent, slot = call(
        send_kernel,
        (
            jax.ShapeDtypeStruct((devices * BLOCK, LANES), BF16),
            jax.ShapeDtypeStruct((1, count), F32),
        ),
        [pltpu.VMEM((devices * BLOCK, LANES), F32)],
        name="send",
        in_specs=[whole, pl.BlockSpec(memory_space=pltpu.SMEM), whole, whole],
    )(coefficients, occupied, positions, spin_labels.reshape(count // LANES, LANES))
    received = lax.all_to_all(sent.reshape(devices, BLOCK, LANES), everyone, 0, 0, tiled=True)
    sorted_features = call(sort_kernel, jax.ShapeDtypeStruct(features.shape, BF16), name="sort")(slot, features)

    chunks = count // LANES
    values = call(
        functools.partial(orbital_kernel, unroll=4, each=each),
        jax.ShapeDtypeStruct((walk_count, 2 * chunks, LANES), F32),
        [
            pltpu.VMEM((4 * HALF, 2 * HALF), F32),
            pltpu.VMEM((4 * HALF, 512), BF16),
            pltpu.VMEM((2, devices, 64, LANES), F32),
            pltpu.VMEM((2, devices, 8, LANES), F32),
            pltpu.SMEM((walk_count * chunks // 2,), jnp.int32),
        ],
        name="orbital",
    )(received, lattice.reshape(2, walk_count, rows))
    target = lax.all_to_all(values, "walk", 0, 0, tiled=True).reshape(-1, LANES)

    spins = occupied.shape[0]
    per_spin = band_count // spins
    spin = band_index // per_spin
    columns = orbital_head.reshape(orbital_head.shape[0], spins, 2, per_spin, each)
    columns = lax.dynamic_index_in_dim(columns, spin, 1, keepdims=False)
    columns = lax.dynamic_index_in_dim(columns, band_index % per_spin, 2, keepdims=False)
    columns = jnp.transpose(columns, (1, 2, 0))
    columns = jnp.pad(columns, ((0, 0), (0, walk_count - each), (0, 0))).reshape(2 * walk_count, -1)
    ups = jnp.sum((spin_labels == 0).astype(jnp.int32))
    place = lax.broadcasted_iota(jnp.int32, (1, count), 1)
    mine = ((place < ups) == (spin == 0)).astype(jnp.int32)
    walkers = walk_count * count // orbitals
    hidden = features.shape[1]
    own = call(
        functools.partial(gradient_kernel, scale=1.0 / walkers),
        jax.ShapeDtypeStruct((2 * walk_count, hidden), F32),
        name="gradient",
    )(target, sorted_features, columns, mine)
    own = own.reshape(2, walk_count, hidden)[:, :each].reshape(-1, LANES)
    shares = lax.all_to_all(jnp.broadcast_to(own, (walk_count, *own.shape)), "walk", 0, 0, tiled=True)
    summed = jnp.sum(shares, axis=0)
    whole = lax.all_to_all(jnp.broadcast_to(summed, (band_count, *own.shape)), "band", 0, 0, tiled=True)
    whole = whole.reshape(spins, per_spin, 2, each, hidden)
    return jnp.transpose(whole, (4, 0, 2, 1, 3)).reshape(hidden, 2 * orbitals)


def solution(mesh):
    return jax.shard_map(
        local,
        mesh=mesh,
        in_specs=(
            P(None, "walk"),
            P(None, "walk", "band"),
            P(),
            P("walk"),
            P(),
            P("walk", None),
            P(),
        ),
        out_specs=P(),
        check_vma=False,
    )
```

time: 122 us -> 107 us (0.88)
  waiting for transfers between devices: 30.6 us -> 22.7 us
  local copies, waits for them, and re-layouts: 12.8 us -> 6.07 us
  blocking collectives: 22.9 us -> 24.6 us
    all_to_all x2, waiting for transfers between devices: 30.6 us -> 22.7 us  [the longest x1 20.1 us: local(): lax.all_to_all(sent.reshape(devices, BLOCK, LANES), everyone, 0, 0, tiled...]
    unnamed x19, local copies, waits for them, and re-layouts: 9.35 us -> 3.22 us
    all_to_all x1, blocking collectives: 13.5 us -> 15.2 us  [local(): lax.all_to_all(jnp.broadcast_to(own, (walk_count, *own.shape)), 'walk', 0...]
    all_to_all x2 -> x0, local copies, waits for them, and re-layouts: 1.67 us -> none  [the longest x1 1.15 us: local(): target = lax.all_to_all(values, 'walk', 0, 0, tiled=True)]
    all_to_all x1 -> x0, other arithmetic: 1.51 us -> none  [local(): received = lax.all_to_all(sent, everyone, 0, 0, tiled=True)]
    transpose x1, local copies, waits for them, and re-layouts: 0.01 us -> 1.33 us  [local(): columns = jnp.transpose(columns, (1, 2, 0))]
    pallas_call x2 -> x3, Pallas kernels: 35.7 us -> 35.1 us  [the longest x1 25.6 us: local(): call(functools.partial(orbital_kernel, unroll=4, each=each), jax.ShapeDty...]
  transfers between devices with their start and end apart: 2 -> 2, of which waited for: 2 -> 2; matrix products, arithmetic and copies ran while one was open for 0% -> 3% of each run, Pallas kernels for 0% -> 6%
where the time goes in v2:
time: 107 us
  Pallas kernels  37 us (35%)
  blocking collectives  24.6 us (23%)
  waiting for transfers between devices  22.7 us (21%)
  starting transfers between devices  14.7 us (14%)
  local copies, waits for them, and re-layouts  6.07 us (6%)
  other arithmetic  1.38 us (1%)
    pallas_call x1, Pallas kernels, local(): call(functools.partial(orbital_kernel, unroll=4, each=each), jax.ShapeDty...  25.6 us
    all_to_all x1, waiting for transfers between devices, local(): lax.all_to_all(sent.reshape(devices, BLOCK, LANES), everyone, 0, 0, tiled...  20.1 us
    all_to_all x1, blocking collectives, local(): lax.all_to_all(jnp.broadcast_to(own, (walk_count, *own.shape)), 'walk', 0...  15.2 us
    all_to_all x1, starting transfers between devices, local(): lax.all_to_all(sent.reshape(devices, BLOCK, LANES), everyone, 0, 0, tiled...  11.2 us
    all_to_all x1, blocking collectives, local(): lax.all_to_all(jnp.broadcast_to(summed, (band_count, *own.shape)), 'band'...  9.34 us
    pallas_call x1, Pallas kernels, local(): call(sort_kernel, jax.ShapeDtypeStruct(features.shape, BF16), name='sort')  6.21 us
    all_to_all x1, starting transfers between devices, local(): target = lax.all_to_all(values, 'walk', 0, 0, tiled=True).reshape(-1, LANES)  3.55 us
    pallas_call x1, Pallas kernels, local(): call(send_kernel, (jax.ShapeDtypeStruct((devices * BLOCK, LANES), BF16),...  3.29 us
  transfers between devices with their start and end apart: 2, of which 2 were waited for; matrix products, arithmetic and copies ran while one was open for 3% of the time, Pallas kernels for 6%

profile of v2, /device:TPU:0, one launch (start us, length us, event | category | flops | bytes accessed | tf_op | source)
XLA Modules:
  0.0 106.6 jit_solution(9873194436115254273)
XLA Ops:
  0.0 0.0 copy-start.1
  0.0 1.1 copy-done.1
  1.1 0.0 copy-start.2
  1.1 0.7 copy-done.2
  1.8 0.7 copy-done.4
  2.5 0.0 copy-start.5
  2.5 0.7 copy-done.5
  3.2 0.0 copy-start.6
  3.2 3.3 %send.1 = (bf16[5120,128]{1,0:T(8,128)(2,1)}, f32[1,3072]{1,0:T(1,128)S(1)}) custom-call(bf16[2,1152,128]{2,1,0:T(8,128)(2,1)S(1)} %copy-done.1, s32[2,48]{1,0:T(2,128)S(1)} %copy-done.5, f32[2,3072]{1,0:T(2,128)S(1)} %copy-done.4, s32[24,128]{1,0:T(8,128)S(1)} %bitcast.23), custom_call_target="tpu_custom_call" | custom-call | tf_op jit(solution)/shard_map/send/pallas_call | solution.py:306
  6.5 0.0 copy-start.7
  6.5 0.0 copy-start.3
  6.5 11.2 %all-to-all-start = ((bf16[128,40,128]{2,1,0:T(8,128)(2,1)}), bf16[128,40,128]{2,1,0:T(8,128)(2,1)S(1)}, u32[]{:S(2)}, u32[]{:S(2)}) async-start(bf16[128,40,128]{2,1,0:T(8,128)(2,1)} %bitcast.1), calls=%async_computation | async-start | bytes 2621440 | tf_op jit(solution)/shard_map/all_to_all | solution.py:316
  17.7 0.0 copy-done.6
  17.7 0.0 copy-start
  17.7 0.0 copy-done.7
  17.7 0.7 reshape.52
  18.4 0.0 copy-done.3
  18.4 0.7 convert_reduce_fusion
  19.1 20.1 %all-to-all-done.recv_ref = bf16[128,40,128]{2,1,0:T(8,128)(2,1)S(1)} async-done(((bf16[128,40,128]{2,1,0:T(8,128)(2,1)}), bf16[128,40,128]{2,1,0:T(8,128)(2,1)S(1)}, u32[]{:S(2)}, u32[]{:S(2)}) %all-to-all-start) | async-done | bytes 1310752 | tf_op jit(solution)/shard_map/all_to_all | solution.py:316
  39.2 25.6 %orbital.1 = f32[16,48,128]{2,1,0:T(8,128)} custom-call(bf16[128,40,128]{2,1,0:T(8,128)(2,1)S(1)} %all-to-all-done.recv_ref, s32[2,16,1152]{2,1,0:T(8,128)S(1)} %bitcast.20), custom_call_target="tpu_custom_call" | custom-call | tf_op jit(solution)/shard_map/orbital/pallas_call | solution.py:320
  64.8 3.6 %all-to-all-start.1 = ((f32[16,48,128]{2,1,0:T(8,128)}), f32[16,48,128]{2,1,0:T(8,128)S(1)}, u32[]{:S(2)}, u32[]{:S(2)}) async-start(f32[16,48,128]{2,1,0:T(8,128)} %orbital.1), calls=%async_computation.1 | async-start | bytes 786432 | tf_op jit(solution)/shard_map/all_to_all | solution.py:332
  68.4 1.3 %dynamic-slice_bitcast_fusion = bf16[2,12,256]{2,1,0:T(8,128)(2,1)} fusion(bf16[256,2,2,4,12]{0,4,3,2,1:T(8,128)(2,1)} %reshape.52, s32[]{:T(128)S(6)} %select_n.25, s32[]{:T(128)S(6)} %select_n.28), kind=kLoop, calls=%fused_computation.2 | loop fusion | bytes 24584 | tf_op jit(solution)/shard_map/transpose | solution.py:340
  69.7 0.0 copy-done
  69.7 6.2 %sort.1.feature_ref = bf16[3072,256]{1,0:T(8,128)(2,1)S(1)} custom-call(f32[1,3072]{1,0:T(1,128)S(1)} %get-tuple-element.8.slot_ref, bf16[3072,256]{1,0:T(8,128)(2,1)S(1)} %copy-done), custom_call_target="tpu_custom_call" | custom-call | tf_op jit(solution)/shard_map/sort/pallas_call | solution.py:317
  75.9 0.0 copy-done.8
  75.9 0.7 compare_convert_fusion.mask_ref
  76.6 2.7 %all-to-all-done.1 = f32[16,48,128]{2,1,0:T(8,128)S(1)} async-done(((f32[16,48,128]{2,1,0:T(8,128)}), f32[16,48,128]{2,1,0:T(8,128)S(1)}, u32[]{:S(2)}, u32[]{:S(2)}) %all-to-all-start.1) | async-done | bytes 393248 | tf_op jit(solution)/shard_map/all_to_all | solution.py:332
  79.3 1.9 %gradient.1 = f32[32,256]{1,0:T(8,128)S(1)} custom-call(f32[768,128]{1,0:T(8,128)S(1)} %bitcast.19, bf16[3072,256]{1,0:T(8,128)(2,1)S(1)} %sort.1.feature_ref, bf16[32,256]{1,0:T(8,128)(2,1)S(1)} %bitcast.22, s32[1,3072]{1,0:T(1,128)S(1)} %compare_convert_fusion.mask_ref), custom_call_target="tpu_custom_call" | custom-call | tf_op jit(solution)/shard_map/gradient/pallas_call | solution.py:347
  81.2 15.2 %all_to_all.20 = f32[16,48,128]{2,1,0:T(8,128)S(1)} all-to-all(f32[16,48,128]{2,1,0:T(8,128)S(1)} %broadcast_in_dim.6), channel_id=1, replica_groups=mesh['walk'=16,'band'=8] {'walk'}, dimensions={0} | all-to-all | bytes 786432 | tf_op jit(solution)/shard_map/all_to_all | solution.py:353
  96.5 9.3 %all_to_all.21 = f32[8,48,128]{2,1,0:T(8,128)S(1)} all-to-all(f32[8,48,128]{2,1,0:T(8,128)S(1)} %broadcast_in_dim.7), channel_id=1, replica_groups=mesh['walk'=16,'band'=8] {'band'}, dimensions={0} | all-to-all | bytes 393216 | tf_op jit(solution)/shard_map/all_to_all | solution.py:355
  105.8 0.1 reshape.56
  105.9 0.7 reshape.57
  (9 shorter events, 0.1 us)
Async XLA Ops:
  0.0 1.1 copy-start.1
  1.1 0.7 copy-start.2
  1.8 0.7 copy-start.4
  2.5 0.7 copy-start.5
  3.2 14.5 %copy-start.6 = (s32[2,18432]{1,0:T(2,128)S(1)}, s32[2,18432]{1,0:T(2,128)}, u32[]{:S(2)}) copy-start(s32[2,18432]{1,0:T(2,128)} %param.9) | copy-start | bytes 442372
  6.5 11.3 %copy-start.7 = (bf16[256,192]{0,1:T(8,128)(2,1)S(1)}, bf16[256,192]{0,1:T(8,128)(2,1)}, u32[]{:S(2)}) copy-start(bf16[256,192]{0,1:T(8,128)(2,1)} %param.13) | copy-start | bytes 294916
  6.5 11.9 %copy-start.3 = (s32[3072]{0:T(1024)S(1)}, s32[3072]{0:T(1024)}, u32[]{:S(2)}) copy-start(s32[3072]{0:T(1024)} %param.10) | copy-start | bytes 36868
  6.5 32.7 %all-to-all-start = ((bf16[128,40,128]{2,1,0:T(8,128)(2,1)}), bf16[128,40,128]{2,1,0:T(8,128)(2,1)S(1)}, u32[]{:S(2)}, u32[]{:S(2)}) async-start(bf16[128,40,128]{2,1,0:T(8,128)(2,1)} %bitcast.1), calls=%async_computation | async-start | bytes 2621440 | tf_op jit(solution)/shard_map/all_to_all | solution.py:316
  17.7 52.0 %copy-start = (bf16[3072,256]{1,0:T(8,128)(2,1)S(1)}, bf16[3072,256]{1,0:T(8,128)(2,1)}, u32[]{:S(2)}) copy-start(bf16[3072,256]{1,0:T(8,128)(2,1)} %feature_ref.1) | copy-start | bytes 4718596
  64.8 14.5 %all-to-all-start.1 = ((f32[16,48,128]{2,1,0:T(8,128)}), f32[16,48,128]{2,1,0:T(8,128)S(1)}, u32[]{:S(2)}, u32[]{:S(2)}) async-start(f32[16,48,128]{2,1,0:T(8,128)} %orbital.1), calls=%async_computation.1 | async-start | bytes 786432 | tf_op jit(solution)/shard_map/all_to_all | solution.py:332
  69.7 6.2 %copy-start.8 = (bf16[2,12,256]{2,1,0:T(8,128)(2,1)S(1)}, bf16[2,12,256]{2,1,0:T(8,128)(2,1)}, u32[]{:S(2)}) copy-start(bf16[2,12,256]{2,1,0:T(8,128)(2,1)} %dynamic-slice_bitcast_fusion) | copy-start | bytes 36868

commit v3 on v2

v3 whole, which is shorter than its diff:
```python
import functools

import jax
import jax.numpy as jnp
from jax import lax
from jax.experimental import pallas as pl
from jax.experimental.pallas import tpu as pltpu
from jax.sharding import PartitionSpec as P


INTERPRET = False
F32 = jnp.float32
BF16 = jnp.bfloat16
PI = 3.141592653589793
BLOCK = 24
RUN = 1024
HALF = 80
LANES = 128


def split3(value):
    high = value.astype(BF16)
    rest = value - high.astype(F32)
    middle = rest.astype(BF16)
    low = (rest - middle.astype(F32)).astype(BF16)
    return high, middle, low


def pick_kernel(coef_hbm, occ_hbm, out_ref, coef_ref, occ_ref, stage_ref, sems):
    copies = [pltpu.make_async_copy(occ_hbm, occ_ref, sems.at[2])]
    copies += [pltpu.make_async_copy(coef_hbm.at[part], coef_ref.at[part], sems.at[part]) for part in range(2)]
    for copy in copies:
        copy.start()
    _, rows, bands = coef_ref.shape
    spins, per_spin = occ_ref.shape
    devices = stage_ref.shape[0] // BLOCK
    senders = lax.axis_size("band")
    each = spins * per_spin // senders
    tiles = rows // LANES
    base = lax.axis_index("band") * bands
    for row in range(2 * tiles, BLOCK):
        stage_ref[pl.ds(row, devices, stride=BLOCK), :] = jnp.zeros((devices, LANES), F32)
    line = lax.broadcasted_iota(jnp.int32, (8, bands), 0)
    lane = lax.broadcasted_iota(jnp.int32, (8, bands), 1) + base
    copies[0].wait()
    picks = []
    for group in range(devices // senders):
        wanted = jnp.full((8, bands), -1, jnp.int32)
        if group < each:
            for sender in range(senders):
                orbital = sender * each + group
                wanted = jnp.where(line == sender, occ_ref[orbital // per_spin, orbital % per_spin], wanted)
        picks.append(jnp.where(lane == wanted, 1.0, 0.0))
    pick = jnp.concatenate(picks, axis=0).astype(BF16)
    for part in range(2):
        copies[1 + part].wait()
        taken = lax.dot_general(
            pick, coef_ref[part], (((1,), (1,)), ((), ())), preferred_element_type=F32
        )
        for tile in range(tiles):
            stage_ref[pl.ds(part * tiles + tile, devices, stride=BLOCK), :] = taken[:, tile * LANES : (tile + 1) * LANES]
    out_ref[...] = stage_ref[...].astype(BF16)


def order_kernel(pos_ref, label_ref, out_ref, slot_ref, up_ref):
    chunks = label_ref.shape[0]
    own = RUN // LANES
    runs = chunks // own
    up = label_ref[...] == 0
    ones = jnp.where(up, 1.0, 0.0)
    row = lax.broadcasted_iota(jnp.int32, (LANES, LANES), 0)
    column = lax.broadcasted_iota(jnp.int32, (LANES, LANES), 1)
    until = jnp.where(row <= column, 1.0, 0.0).astype(BF16)
    inside = jnp.dot(ones.astype(BF16), until, preferred_element_type=F32)
    whole = jnp.broadcast_to(inside[:, LANES - 1 : LANES], inside.shape).astype(BF16)
    row = lax.broadcasted_iota(jnp.int32, (chunks, chunks), 0)
    column = lax.broadcasted_iota(jnp.int32, (chunks, chunks), 1)
    same = jnp.where(row // own == column // own, 1.0, 0.0)
    before = jnp.where(column < row, same, 0.0).astype(BF16)
    rank = inside + jnp.dot(before, whole, preferred_element_type=F32)
    total = jnp.dot(same.astype(BF16), whole, preferred_element_type=F32)
    place = (
        lax.broadcasted_iota(jnp.int32, rank.shape, 0) % own * LANES + lax.broadcasted_iota(jnp.int32, rank.shape, 1)
    ).astype(F32)
    slot = jnp.where(up, rank - 1.0, total + place - rank)
    first = jnp.where(place < total, 1.0, 0.0)
    up_ref[...] = jnp.concatenate([first[chunk : chunk + 1, :] for chunk in range(chunks)], axis=1)
    parts = jnp.concatenate([part.astype(F32) for part in split3(pos_ref[...])], axis=0).astype(BF16)
    here = lax.broadcasted_iota(jnp.int32, (RUN, RUN), 0).astype(F32)
    for run in range(runs):
        line = jnp.concatenate([slot[run * own + k : run * own + k + 1, :] for k in range(own)], axis=1)
        slot_ref[run : run + 1, :] = line
        move = jnp.where(here == line, 1.0, 0.0).astype(BF16)
        moved = lax.dot_general(
            parts[:, run * RUN : (run + 1) * RUN], move, (((1,), (1,)), ((), ())), preferred_element_type=F32
        )
        moved = moved[0:2] + moved[2:4] + moved[4:6]
        for axis in range(2):
            for k in range(own):
                at = axis * chunks + run * own + k
                out_ref[at : at + 1, :] = moved[axis : axis + 1, k * LANES : (k + 1) * LANES]
        out_ref[2 * chunks + run : 2 * chunks + run + 1, :] = total[run * own : run * own + 1, :]
    out_ref[2 * chunks + runs :, :] = jnp.zeros((out_ref.shape[0] - 2 * chunks - runs, LANES), F32)


def sort_kernel(slot_ref, feature_ref, out_ref):
    here = lax.broadcasted_iota(jnp.int32, (RUN, RUN), 0).astype(F32)
    for run in range(slot_ref.shape[0]):
        move = jnp.where(here == slot_ref[run : run + 1, :], 1.0, 0.0).astype(BF16)
        moved = jnp.dot(move, feature_ref[run * RUN : (run + 1) * RUN, :], preferred_element_type=F32)
        out_ref[run * RUN : (run + 1) * RUN, :] = moved.astype(BF16)


def base_wave(turns):
    quarter = (turns - 0.5) * (0.5 * PI)
    square = quarter * quarter
    sine = quarter * (
        1.0 + square * (-1 / 6 + square * (1 / 120 + square * (-1 / 5040 + square * (1 / 362880))))
    )
    cosine = 1.0 + square * (
        -1 / 2 + square * (1 / 24 + square * (-1 / 720 + square * (1 / 40320 - square * (1 / 3628800))))
    )
    sine, cosine = 2.0 * sine * cosine, 1.0 - 2.0 * sine * sine
    sine, cosine = 2.0 * sine * cosine, 1.0 - 2.0 * sine * sine
    return -cosine, -sine


def times(left, right):
    return left[0] * right[0] - left[1] * right[1], left[1] * right[0] + left[0] * right[1]


def fold_kernel(recv_ref, lat_ref, table_ref, sum_ref):
    groups = lat_ref.shape[1]
    senders = recv_ref.shape[0] // groups
    rows = lat_ref.shape[2]
    tiles = rows // LANES

    sum_ref[...] = jnp.zeros_like(sum_ref)
    frequency = lax.broadcasted_iota(jnp.int32, (HALF, rows), 0)

    def fold(group, carry):
        both = recv_ref[group * senders].astype(F32)
        for sender in range(1, senders):
            both = both + recv_ref[group * senders + sender].astype(F32)
        c_real, c_imag = (jnp.concatenate([both[k + t : k + t + 1] for t in range(tiles)], axis=1) for k in (0, tiles))
        lat_a = lat_ref[0, pl.ds(group, 1), :]
        lat_b = lat_ref[1, pl.ds(group, 1), :]
        sign_a = jnp.where(lat_a < 0, -1.0, 1.0)
        sign_b = jnp.where(lat_b < 0, -1.0, 1.0)
        at_a = frequency == jnp.abs(lat_a)
        at_b = frequency == jnp.abs(lat_b)
        zero = jnp.zeros((), F32)
        left = jnp.concatenate(
            [
                jnp.where(at_a, value, zero).astype(BF16)
                for value in (c_real, c_real * sign_a, c_imag, c_imag * sign_a)
            ],
            axis=0,
        )
        right = jnp.concatenate(
            [jnp.where(at_b, value, zero).astype(BF16) for value in (jnp.ones_like(sign_b), sign_b)], axis=0
        )
        sum_ref[...] += lax.dot_general(left, right, (((1,), (1,)), ((), ())), preferred_element_type=F32)
        return carry

    lax.fori_loop(0, groups, fold, 0, unroll=4)
    real_even = sum_ref[0:HALF, :]
    real_odd = sum_ref[HALF : 2 * HALF, :]
    imag_even = sum_ref[2 * HALF : 3 * HALF, :]
    imag_odd = sum_ref[3 * HALF : 4 * HALF, :]
    even = lax.broadcasted_iota(jnp.int32, real_even.shape, 1) < HALF
    table = jnp.concatenate(
        [
            jnp.where(even, real_even, -imag_even),
            jnp.where(even, -imag_odd, -real_odd),
            jnp.where(even, imag_even, real_even),
            jnp.where(even, real_odd, -imag_odd),
        ],
        axis=0,
    )
    high = table.astype(BF16).astype(F32)
    low = table - high
    pad = jnp.zeros((4 * HALF, table_ref.shape[1] - 6 * HALF), F32)
    table_ref[...] = jnp.concatenate([high, high, low, pad], axis=1).astype(BF16)


def orbital_kernel(table_ref, pos_ref, out_ref, wave_ref, eight_ref, list_ref, *, unroll, each):
    groups = out_ref.shape[0]
    chunks = out_ref.shape[1] // 2
    own = RUN // LANES
    runs = chunks // own
    upper = lax.axis_index("band") < lax.axis_size("band") // 2
    walk = lax.axis_index("walk")
    active = walk < each
    out_ref[...] = jnp.zeros_like(out_ref)

    def waves(group, length):
        away = group ^ walk
        for line in range(0, 2 * chunks, 8):
            first = base_wave(pos_ref[away, line : line + 8, :])
            power = (jnp.ones((8, LANES), F32), jnp.zeros((8, LANES), F32))
            for k in range(8):
                for half in range(2):
                    wave_ref[half, group, pl.ds(line * 8 + k, 8, stride=8), :] = power[half]
                power = first if k == 0 else times(power, first)
            for half in range(2):
                eight_ref[half, group, line : line + 8, :] = power[half]
        numbers = pos_ref[away, 2 * chunks : 2 * chunks + runs, :].astype(jnp.int32)
        for run in range(runs):
            number = numbers[run, 0]
            low = jnp.where(upper, 0, number // LANES)
            high = jnp.where(upper, (number + LANES - 1) // LANES, own)
            high = jnp.where(active, high, low)

            def note(chunk, at):
                list_ref[at] = group * chunks + run * own + chunk
                return at + 1

            length = lax.fori_loop(low, high, note, length)
        return length

    length = lax.fori_loop(0, groups, waves, 0)

    def basis(entry, axis):
        group = entry // chunks
        line = axis * chunks + entry % chunks
        start = pl.multiple_of(line * 8, 8)
        now = tuple(wave_ref[half, group, pl.ds(start, 8), :] for half in range(2))
        step = tuple(jnp.broadcast_to(eight_ref[half, group, pl.ds(line, 1), :], (8, LANES)) for half in range(2))
        twice = 2.0 * step[0]
        last, now = now, times(now, step)
        cosines, sines = [last[0], now[0]], [last[1], now[1]]
        for _ in range(2, HALF // 8):
            last, now = now, tuple(twice * now[half] - last[half] for half in range(2))
            cosines.append(now[0])
            sines.append(now[1])
        return jnp.concatenate(cosines + sines, axis=0)

    zeros = jnp.zeros((table_ref.shape[1] - 6 * HALF, 2 * LANES), BF16)

    def evaluate(index, carry):
        for inner in range(unroll):
            entries = [
                list_ref[jnp.minimum((index * unroll + inner) * 2 + side, length - 1)] for side in range(2)
            ]
            wave_y = jnp.concatenate([basis(entry, 1) for entry in entries], axis=1)
            high_y = wave_y.astype(BF16)
            low_y = (wave_y - high_y.astype(F32)).astype(BF16)
            weights = jnp.concatenate([high_y, low_y, high_y, zeros], axis=0)
            inside = jnp.dot(table_ref[...], weights, preferred_element_type=F32)
            wave_x = jnp.concatenate([basis(entry, 0) for entry in entries], axis=1)
            for half in range(2):
                value = jnp.sum(inside[half * 2 * HALF : (half + 1) * 2 * HALF, :] * wave_x, axis=0, keepdims=True)
                for side, entry in enumerate(entries):
                    out_ref[entry // chunks, pl.ds(half * chunks + entry % chunks, 1), :] = value[:, side * LANES : (side + 1) * LANES]
        return carry

    lax.fori_loop(0, (length + 2 * unroll - 1) // (2 * unroll), evaluate, 0)


def gradient_kernel(target_ref, feature_ref, head_ref, up_ref, out_ref, *, scale):
    count = feature_ref.shape[0]
    chunks = count // LANES
    slots = head_ref.shape[0] // 2
    features = feature_ref[...]
    net = lax.dot_general(head_ref[...], features, (((1,), (1,)), ((), ())), preferred_element_type=F32)
    upper = lax.axis_index("band") < lax.axis_size("band") // 2
    mine = up_ref[...] == jnp.where(upper, 1.0, 0.0)
    parts = []
    for half in range(2):
        target = jnp.concatenate(
            [target_ref[pl.ds(half * chunks + chunk, slots, stride=2 * chunks), :] for chunk in range(chunks)], axis=1
        )
        scaled = (net[half * slots : (half + 1) * slots, :] - target) * scale
        parts.append(jnp.where(mine, scaled, 0.0))
    spread = jnp.concatenate(parts, axis=0)
    total = jnp.zeros(out_ref.shape, F32)
    for piece in split3(spread):
        total = total + jnp.dot(piece, features, preferred_element_type=F32)
    out_ref[...] = total


def call(kernel, out, scratch=(), **more):
    return pl.pallas_call(
        kernel,
        out_shape=out,
        **more,
        scratch_shapes=list(scratch),
        interpret=INTERPRET,
        compiler_params=pltpu.CompilerParams(vmem_limit_bytes=48 * 1024 * 1024),
    )


def local(positions, coefficients, lattice, spin_labels, occupied, features, orbital_head):
    walk_count = lax.axis_size("walk")
    band_count = lax.axis_size("band")
    band_index = lax.axis_index("band")
    devices = walk_count * band_count
    rows = coefficients.shape[1]
    count = positions.shape[1]
    orbitals = occupied.shape[0] * occupied.shape[1]
    each = orbitals // band_count

    chunks = count // LANES
    anywhere = pl.BlockSpec(memory_space=pl.ANY)
    picked = call(
        pick_kernel,
        jax.ShapeDtypeStruct((devices * BLOCK, LANES), BF16),
        [
            pltpu.VMEM(coefficients.shape, BF16),
            pltpu.SMEM(occupied.shape, jnp.int32),
            pltpu.VMEM((devices * BLOCK, LANES), F32),
            pltpu.SemaphoreType.DMA((3,)),
        ],
        in_specs=[anywhere, anywhere],
    )(coefficients, occupied)
    picked, positions = lax.optimization_barrier((picked, positions))
    received = lax.all_to_all(picked.reshape(devices, BLOCK, LANES), ("walk", "band"), 0, 0, tiled=True)
    ordered, slot, up = call(
        order_kernel,
        (
            jax.ShapeDtypeStruct((2 * chunks + 8, LANES), F32),
            jax.ShapeDtypeStruct((count // RUN, RUN), F32),
            jax.ShapeDtypeStruct((1, count), F32),
        ),
    )(positions, spin_labels.reshape(chunks, LANES))
    everyone = ordered[None]
    for flips in ((1,), (2, 4, 6), (8,)):
        moved = [lax.ppermute(everyone, "walk", [(k, k ^ flip) for k in range(walk_count)]) for flip in flips]
        everyone = jnp.concatenate([everyone, *moved], axis=0)
    sorted_features = call(sort_kernel, jax.ShapeDtypeStruct(features.shape, BF16))(slot, features)
    table = call(
        fold_kernel, jax.ShapeDtypeStruct((4 * HALF, 512), BF16), [pltpu.VMEM((4 * HALF, 2 * HALF), F32)]
    )(received, lattice.reshape(2, walk_count, rows))
    values = call(
        functools.partial(orbital_kernel, unroll=8, each=each),
        jax.ShapeDtypeStruct((walk_count, 2 * chunks, LANES), F32),
        [
            pltpu.VMEM((2, walk_count, 16 * chunks, LANES), F32),
            pltpu.VMEM((2, walk_count, 2 * chunks, LANES), F32),
            pltpu.SMEM((walk_count * chunks,), jnp.int32),
        ],
    )(table, everyone)
    target = lax.all_to_all(values, "walk", 0, 0, tiled=True).reshape(-1, LANES)

    spins = occupied.shape[0]
    per_spin = band_count // spins
    spin = band_index // per_spin
    columns = orbital_head.reshape(orbital_head.shape[0], spins, 2, per_spin, each)
    columns = lax.dynamic_index_in_dim(columns, spin, 1, keepdims=False)
    columns = lax.dynamic_index_in_dim(columns, band_index % per_spin, 2, keepdims=False)
    columns = jnp.transpose(columns, (1, 2, 0))
    columns = jnp.pad(columns, ((0, 0), (0, walk_count - each), (0, 0))).reshape(2 * walk_count, -1)
    walkers = walk_count * count // orbitals
    hidden = features.shape[1]
    own = call(
        functools.partial(gradient_kernel, scale=1.0 / walkers), jax.ShapeDtypeStruct((2 * walk_count, hidden), F32)
    )(target, sorted_features, columns, up)
    own = own.reshape(2, walk_count, hidden)[:, :each].reshape(-1, LANES)
    own = own + lax.ppermute(own, "walk", [(k, k ^ 1) for k in range(walk_count)])
    chips = walk_count // 2
    shares = lax.all_to_all(
        jnp.broadcast_to(own, (chips, *own.shape)),
        "walk",
        0,
        0,
        axis_index_groups=[[2 * chip + core for chip in range(chips)] for core in range(2)],
        tiled=True,
    )
    summed = jnp.sum(shares, axis=0)
    whole = lax.all_to_all(jnp.broadcast_to(summed, (band_count, *own.shape)), "band", 0, 0, tiled=True)
    whole = whole.reshape(spins, per_spin, 2, each, hidden)
    return jnp.transpose(whole, (4, 0, 2, 1, 3)).reshape(hidden, 2 * orbitals)


def solution(mesh):
    return jax.shard_map(
        local,
        mesh=mesh,
        in_specs=(
            P(None, "walk"),
            P(None, "walk", "band"),
            P(),
            P("walk"),
            P(),
            P("walk", None),
            P(),
        ),
        out_specs=P(),
        check_vma=False,
    )
```

time: 107 us -> 104 us (0.972)
  starting transfers between devices: 14.7 us -> 21 us
  Pallas kernels: 37 us -> 30.9 us
  waiting for transfers between devices: 22.7 us -> 25.7 us
  blocking collectives: 24.6 us -> 21.9 us
  local copies, waits for them, and re-layouts: 6.07 us -> 4.13 us
  other arithmetic: 1.38 us -> 0.03 us
    all_to_all x1, waiting for transfers between devices: 20.1 us -> 0.01 us  [local(): lax.all_to_all(picked.reshape(devices, BLOCK, LANES), ('walk', 'band'), 0...]
    ppermute x0 -> x6, waiting for transfers between devices: none -> 17.4 us  [the longest x5 16.3 us: local(): lax.ppermute(everyone, 'walk', [(k, k ^ flip) for k in range(walk_count)])]
    ppermute x0 -> x6, starting transfers between devices: none -> 6.26 us  [the longest x5 6.17 us: local(): lax.ppermute(everyone, 'walk', [(k, k ^ flip) for k in range(walk_count)])]
    pallas_call x3 -> x5, Pallas kernels: 35.1 us -> 29 us  [the longest x1 18.4 us: local(): call(functools.partial(orbital_kernel, unroll=8, each=each), jax.ShapeDty...]
    all_to_all x1, waiting for transfers between devices: 2.65 us -> 8.26 us  [local(): target = lax.all_to_all(values, 'walk', 0, 0, tiled=True).reshape(-1, LANES)]
    all_to_all x1, blocking collectives: 15.2 us -> 11.1 us  [local(): lax.all_to_all(jnp.broadcast_to(own, (chips, *own.shape)), 'walk', 0, 0,...]
    all_to_all x1, blocking collectives: 9.34 us -> 10.8 us  [local(): lax.all_to_all(jnp.broadcast_to(summed, (band_count, *own.shape)), 'band'...]
    transpose x1, local copies, waits for them, and re-layouts: 1.33 us -> 0.01 us  [local(): columns = jnp.transpose(columns, (1, 2, 0))]
  transfers between devices with their start and end apart: 2 -> 8, of which waited for: 2 -> 7; matrix products, arithmetic and copies ran while one was open for 3% -> 0% of each run, Pallas kernels for 6% -> 4%
where the time goes in v3:
time: 104 us
  Pallas kernels  30.9 us (30%)
  waiting for transfers between devices  25.7 us (25%)
  blocking collectives  21.9 us (21%)
  starting transfers between devices  21 us (20%)
  local copies, waits for them, and re-layouts  4.13 us (4%)
    pallas_call x1, Pallas kernels, local(): call(functools.partial(orbital_kernel, unroll=8, each=each), jax.ShapeDty...  18.4 us
    ppermute x5, waiting for transfers between devices, local(): lax.ppermute(everyone, 'walk', [(k, k ^ flip) for k in range(walk_count)])  16.3 us
    all_to_all x1, starting transfers between devices, local(): lax.all_to_all(picked.reshape(devices, BLOCK, LANES), ('walk', 'band'), 0...  11.2 us
    all_to_all x1, blocking collectives, local(): lax.all_to_all(jnp.broadcast_to(own, (chips, *own.shape)), 'walk', 0, 0,...  11.1 us
    all_to_all x1, blocking collectives, local(): lax.all_to_all(jnp.broadcast_to(summed, (band_count, *own.shape)), 'band'...  10.8 us
    all_to_all x1, waiting for transfers between devices, local(): target = lax.all_to_all(values, 'walk', 0, 0, tiled=True).reshape(-1, LANES)  8.26 us
    ppermute x5, starting transfers between devices, local(): lax.ppermute(everyone, 'walk', [(k, k ^ flip) for k in range(walk_count)])  6.17 us
    pallas_call x1, Pallas kernels, local(): call(fold_kernel, jax.ShapeDtypeStruct((4 * HALF, 512), BF16), [pltpu.VME...  4.74 us
  transfers between devices with their start and end apart: 8, of which 7 were waited for; matrix products, arithmetic and copies ran while one was open for 0% of the time, Pallas kernels for 4%

profile of v3, /device:TPU:0, one launch (start us, length us, event | category | flops | bytes accessed | tf_op | source)
XLA Modules:
  0.0 103.9 jit_solution(18212211512908565090)
XLA Ops:
  0.0 1.1 %copy-done.1 = bf16[2,1152,128]{2,1,0:T(8,128)(2,1)S(1)} copy-done((bf16[2,1152,128]{2,1,0:T(8,128)(2,1)S(1)}, bf16[2,1152,128]{2,1,0:T(8,128)(2,1)}, u32[]{:S(2)}) %copy-start.1) | copy-done | bytes 589848
  1.1 0.7 copy-done.8
  1.8 2.1 %shard_map.73 = bf16[3072,128]{1,0:T(8,128)(2,1)} custom-call(bf16[2,1152,128]{2,1,0:T(8,128)(2,1)S(1)} %copy-done.1, s32[2,48]{1,0:T(2,128)S(1)} %copy-done.8), custom_call_target="tpu_custom_call" | custom-call | tf_op jit(solution)/shard_map/pallas_call | solution.py:306
  3.8 11.2 %all-to-all-start = ((bf16[128,24,128]{2,1,0:T(8,128)(2,1)}), bf16[128,24,128]{2,1,0:T(8,128)(2,1)S(1)}, u32[]{:S(2)}, u32[]{:S(2)}) async-start(bf16[128,24,128]{2,1,0:T(8,128)(2,1)} %bitcast), calls=%async_computation | async-start | bytes 1572864 | tf_op jit(solution)/shard_map/all_to_all | solution.py:318
  15.0 2.1 %shard_map.75 = (f32[56,128]{1,0:T(8,128)S(1)}, f32[3,1024]{1,0:T(4,128)S(1)}, f32[1,3072]{1,0:T(1,128)S(1)}) custom-call(f32[2,3072]{1,0:T(2,128)S(1)} %copy-done.2, s32[24,128]{1,0:T(8,128)S(1)} %bitcast.28), custom_call_target="tpu_custom_call" | custom-call | tf_op jit(solution)/shard_map/pallas_call | solution.py:319
  17.1 0.0 copy-start.5
  17.1 0.1 collective-permute-start
  17.2 1.2 %collective-permute-done = f32[1,56,128]{2,1,0:T(8,128)S(1)} collective-permute-done((f32[1,56,128]{2,1,0:T(8,128)S(1)}, f32[1,56,128]{2,1,0:T(8,128)S(1)}, u32[]{:S(2)}, u32[]{:S(2)}) %collective-permute-start) | collective-permute-done | bytes 28704 | tf_op jit(solution)/shard_map/ppermute | solution.py:329
  18.4 2.8 %collective-permute-start.3 = (f32[2,56,128]{2,1,0:T(8,128)S(1)}, f32[2,56,128]{2,1,0:T(8,128)S(1)}, u32[]{:S(2)}, u32[]{:S(2)}) collective-permute-start(f32[2,56,128]{2,1,0:T(8,128)S(1)} %pad_maximum_fusion), channel_id=1, source_target_pairs={{0,48},{8,56},{16,32},{24,40},{32,16},{40,24},{48,0},{56,8},{64,11... | collective-permute-start | bytes 172040 | tf_op jit(solution)/shard_map/ppermute | solution.py:329
  21.2 0.3 collective-permute-start.2
  21.6 0.9 collective-permute-start.1
  22.5 6.2 %collective-permute-done.1 = f32[2,56,128]{2,1,0:T(8,128)S(1)} collective-permute-done((f32[2,56,128]{2,1,0:T(8,128)S(1)}, f32[2,56,128]{2,1,0:T(8,128)S(1)}, u32[]{:S(2)}, u32[]{:S(2)}) %collective-permute-start.1) | collective-permute-done | bytes 57376 | tf_op jit(solution)/shard_map/ppermute | solution.py:329
  28.7 1.5 %collective-permute-done.2 = f32[2,56,128]{2,1,0:T(8,128)S(1)} collective-permute-done((f32[2,56,128]{2,1,0:T(8,128)S(1)}, f32[2,56,128]{2,1,0:T(8,128)S(1)}, u32[]{:S(2)}, u32[]{:S(2)}) %collective-permute-start.2) | collective-permute-done | bytes 57376 | tf_op jit(solution)/shard_map/ppermute | solution.py:329
  30.2 0.4 collective-permute-done.3
  30.6 2.0 %collective-permute-start.4 = (f32[8,56,128]{2,1,0:T(8,128)S(1)}, f32[8,56,128]{2,1,0:T(8,128)S(1)}, u32[]{:S(2)}, u32[]{:S(2)}) collective-permute-start(f32[8,56,128]{2,1,0:T(8,128)S(1)} %get-tuple-element.15), channel_id=1, source_target_pairs={{0,64},{8,72},{16,80},{24,88},{32,96},{40,104},{48,112},{56,120},{... | collective-permute-start | bytes 688136 | tf_op jit(solution)/shard_map/ppermute | solution.py:329
  32.6 7.0 %collective-permute-done.4 = f32[8,56,128]{2,1,0:T(8,128)S(1)} collective-permute-done((f32[8,56,128]{2,1,0:T(8,128)S(1)}, f32[8,56,128]{2,1,0:T(8,128)S(1)}, u32[]{:S(2)}, u32[]{:S(2)}) %collective-permute-start.4) | collective-permute-done | bytes 229408 | tf_op jit(solution)/shard_map/ppermute | solution.py:329
  39.7 0.0 copy-start.10
  39.7 0.0 copy-start
  39.7 4.7 %shard_map.74.table_ref = bf16[320,512]{1,0:T(8,128)(2,1)S(1)} custom-call(bf16[128,24,128]{2,1,0:T(8,128)(2,1)S(1)} %all-to-all-done.recv_ref, s32[2,16,1152]{2,1,0:T(8,128)S(1)} %bitcast.23), custom_call_target="tpu_custom_call" | custom-call | tf_op jit(solution)/shard_map/pallas_call | solution.py:332
  44.5 18.4 %shard_map.76 = f32[16,48,128]{2,1,0:T(8,128)} custom-call(bf16[320,512]{1,0:T(8,128)(2,1)S(1)} %shard_map.74.table_ref, f32[16,56,128]{2,1,0:T(8,128)S(1)} %constant_dynamic-update-slice_fusion.5.pos_ref), custom_call_target="tpu_custom_call" | custom-call | tf_op jit(solution)/shard_map/pallas_call | solution.py:335
  62.8 3.6 %all-to-all-start.1 = ((f32[16,48,128]{2,1,0:T(8,128)}), f32[16,48,128]{2,1,0:T(8,128)S(1)}, u32[]{:S(2)}, u32[]{:S(2)}) async-start(f32[16,48,128]{2,1,0:T(8,128)} %shard_map.76), calls=%async_computation.1 | async-start | bytes 786432 | tf_op jit(solution)/shard_map/all_to_all | solution.py:344
  66.5 0.7 copy-done.4
  67.2 1.8 %shard_map.77.feature_ref = bf16[3072,256]{1,0:T(8,128)(2,1)S(1)} custom-call(f32[3,1024]{1,0:T(4,128)S(1)} %copy-done.4, bf16[3072,256]{1,0:T(8,128)(2,1)S(1)} %copy-done), custom_call_target="tpu_custom_call" | custom-call | tf_op jit(solution)/shard_map/pallas_call | solution.py:331
  69.0 8.3 %all-to-all-done.1 = f32[16,48,128]{2,1,0:T(8,128)S(1)} async-done(((f32[16,48,128]{2,1,0:T(8,128)}), f32[16,48,128]{2,1,0:T(8,128)S(1)}, u32[]{:S(2)}, u32[]{:S(2)}) %all-to-all-start.1) | async-done | bytes 393248 | tf_op jit(solution)/shard_map/all_to_all | solution.py:344
  77.3 0.7 copy-done.6
  78.0 1.9 %shard_map.78 = f32[32,256]{1,0:T(8,128)S(1)} custom-call(f32[768,128]{1,0:T(8,128)S(1)} %bitcast.22, bf16[3072,256]{1,0:T(8,128)(2,1)S(1)} %shard_map.77.feature_ref, bf16[32,256]{1,0:T(8,128)(2,1)S(1)} %bitcast.27, f32[1,3072]{1,0:T(1,128)S(1)} %copy-done.6), custom_call_target="tpu_custom_call" | custom-call | tf_op jit(solution)/shard_map/pallas_call | solution.py:356
  79.9 0.1 collective-permute-start.5
  80.0 1.2 %collective-permute-done.5 = f32[48,128]{1,0:T(8,128)S(1)} collective-permute-done((f32[48,128]{1,0:T(8,128)S(1)}, f32[48,128]{1,0:T(8,128)S(1)}, u32[]{:S(2)}, u32[]{:S(2)}) %collective-permute-start.5) | collective-permute-done | bytes 24608 | tf_op jit(solution)/shard_map/ppermute | solution.py:360
  81.2 11.1 %all_to_all.20 = f32[8,48,128]{2,1,0:T(8,128)S(1)} all-to-all(f32[8,48,128]{2,1,0:T(8,128)S(1)} %broadcast_in_dim.10), channel_id=1, replica_groups={{0,16,32,48,64,80,96,112},{8,24,40,56,72,88,104,120},{1,17,33,49,65,81,..., dimensions={0} | all-to-all | bytes 393216 | tf_op jit(solution)/shard_map/all_to_all | solution.py:362
  92.3 10.8 %all_to_all.21 = f32[8,48,128]{2,1,0:T(8,128)S(1)} all-to-all(f32[8,48,128]{2,1,0:T(8,128)S(1)} %broadcast_in_dim.11), channel_id=1, replica_groups=mesh['walk'=16,'band'=8] {'band'}, dimensions={0} | all-to-all | bytes 393216 | tf_op jit(solution)/shard_map/all_to_all | solution.py:371
  103.1 0.1 reshape.40
  103.2 0.7 reshape.41
  (33 shorter events, 0.2 us)
Async XLA Ops:
  0.0 1.1 %copy-start.1 = (bf16[2,1152,128]{2,1,0:T(8,128)(2,1)S(1)}, bf16[2,1152,128]{2,1,0:T(8,128)(2,1)}, u32[]{:S(2)}) copy-start(bf16[2,1152,128]{2,1,0:T(8,128)(2,1)} %coef_hbm.1) | copy-start | bytes 1769476
  1.1 0.7 copy-start.8
  1.7 13.3 %copy-start.2 = (f32[2,3072]{1,0:T(2,128)S(1)}, f32[2,3072]{1,0:T(2,128)}, u32[]{:S(2)}) copy-start(f32[2,3072]{1,0:T(2,128)} %pos_ref) | copy-start | bytes 73732
  1.7 13.3 %copy-start.7 = (s32[3072]{0:T(1024)S(1)}, s32[3072]{0:T(1024)}, u32[]{:S(2)}) copy-start(s32[3072]{0:T(1024)} %param.10) | copy-start | bytes 36868
  1.7 30.9 %copy-start.9 = (s32[2,18432]{1,0:T(2,128)S(1)}, s32[2,18432]{1,0:T(2,128)}, u32[]{:S(2)}) copy-start(s32[2,18432]{1,0:T(2,128)} %param.9) | copy-start | bytes 442372
  3.8 35.9 %all-to-all-start = ((bf16[128,24,128]{2,1,0:T(8,128)(2,1)}), bf16[128,24,128]{2,1,0:T(8,128)(2,1)S(1)}, u32[]{:S(2)}, u32[]{:S(2)}) async-start(bf16[128,24,128]{2,1,0:T(8,128)(2,1)} %bitcast), calls=%async_computation | async-start | bytes 1572864 | tf_op jit(solution)/shard_map/all_to_all | solution.py:318
  17.1 22.5 %copy-start.3 = (f32[3,1024]{1,0:T(4,128)}, f32[3,1024]{1,0:T(4,128)S(1)}, u32[]{:S(2)}) copy-start(f32[3,1024]{1,0:T(4,128)S(1)} %get-tuple-element.13.slot_ref) | copy-start | bytes 36868
  17.1 22.5 %copy-start.5 = (f32[1,3072]{1,0:T(1,128)}, f32[1,3072]{1,0:T(1,128)S(1)}, u32[]{:S(2)}) copy-start(f32[1,3072]{1,0:T(1,128)S(1)} %get-tuple-element.14.up_ref) | copy-start | bytes 36868
  17.1 1.3 %collective-permute-start = (f32[1,56,128]{2,1,0:T(8,128)S(1)}, f32[1,56,128]{2,1,0:T(8,128)S(1)}, u32[]{:S(2)}, u32[]{:S(2)}) collective-permute-start(f32[1,56,128]{2,1,0:T(8,128)S(1)} %bitcast.25), channel_id=1, source_target_pairs={{0,8},{8,0},{16,24},{24,16},{32,40},{40,32},{48,56},{56,48},{64,72... | collective-permute-start | bytes 86024 | tf_op jit(solution)/shard_map/ppermute | solution.py:329
  18.4 12.2 %collective-permute-start.3 = (f32[2,56,128]{2,1,0:T(8,128)S(1)}, f32[2,56,128]{2,1,0:T(8,128)S(1)}, u32[]{:S(2)}, u32[]{:S(2)}) collective-permute-start(f32[2,56,128]{2,1,0:T(8,128)S(1)} %pad_maximum_fusion), channel_id=1, source_target_pairs={{0,48},{8,56},{16,32},{24,40},{32,16},{40,24},{48,0},{56,8},{64,11... | collective-permute-start | bytes 172040 | tf_op jit(solution)/shard_map/ppermute | solution.py:329
  21.2 9.0 %collective-permute-start.2 = (f32[2,56,128]{2,1,0:T(8,128)S(1)}, f32[2,56,128]{2,1,0:T(8,128)S(1)}, u32[]{:S(2)}, u32[]{:S(2)}) collective-permute-start(f32[2,56,128]{2,1,0:T(8,128)S(1)} %pad_maximum_fusion), channel_id=1, source_target_pairs={{0,32},{8,40},{16,48},{24,56},{32,0},{40,8},{48,16},{56,24},{64,96... | collective-permute-start | bytes 172040 | tf_op jit(solution)/shard_map/ppermute | solution.py:329
  21.6 7.1 %collective-permute-start.1 = (f32[2,56,128]{2,1,0:T(8,128)S(1)}, f32[2,56,128]{2,1,0:T(8,128)S(1)}, u32[]{:S(2)}, u32[]{:S(2)}) collective-permute-start(f32[2,56,128]{2,1,0:T(8,128)S(1)} %pad_maximum_fusion), channel_id=1, source_target_pairs={{0,16},{8,24},{16,0},{24,8},{32,48},{40,56},{48,32},{56,40},{64,80... | collective-permute-start | bytes 172040 | tf_op jit(solution)/shard_map/ppermute | solution.py:329
  30.6 9.0 %collective-permute-start.4 = (f32[8,56,128]{2,1,0:T(8,128)S(1)}, f32[8,56,128]{2,1,0:T(8,128)S(1)}, u32[]{:S(2)}, u32[]{:S(2)}) collective-permute-start(f32[8,56,128]{2,1,0:T(8,128)S(1)} %get-tuple-element.15), channel_id=1, source_target_pairs={{0,64},{8,72},{16,80},{24,88},{32,96},{40,104},{48,112},{56,120},{... | collective-permute-start | bytes 688136 | tf_op jit(solution)/shard_map/ppermute | solution.py:329
  39.7 26.7 %copy-start.10 = (bf16[256,192]{0,1:T(8,128)(2,1)S(1)}, bf16[256,192]{0,1:T(8,128)(2,1)}, u32[]{:S(2)}) copy-start(bf16[256,192]{0,1:T(8,128)(2,1)} %param.13) | copy-start | bytes 294916
  39.7 26.8 %copy-start = (bf16[3072,256]{1,0:T(8,128)(2,1)S(1)}, bf16[3072,256]{1,0:T(8,128)(2,1)}, u32[]{:S(2)}) copy-start(bf16[3072,256]{1,0:T(8,128)(2,1)} %feature_ref.1) | copy-start | bytes 4718596
  62.8 14.5 %all-to-all-start.1 = ((f32[16,48,128]{2,1,0:T(8,128)}), f32[16,48,128]{2,1,0:T(8,128)S(1)}, u32[]{:S(2)}, u32[]{:S(2)}) async-start(f32[16,48,128]{2,1,0:T(8,128)} %shard_map.76), calls=%async_computation.1 | async-start | bytes 786432 | tf_op jit(solution)/shard_map/all_to_all | solution.py:344
  66.5 0.7 copy-start.4
  77.3 0.7 copy-start.6
  79.9 1.3 %collective-permute-start.5 = (f32[48,128]{1,0:T(8,128)S(1)}, f32[48,128]{1,0:T(8,128)S(1)}, u32[]{:S(2)}, u32[]{:S(2)}) collective-permute-start(f32[48,128]{1,0:T(8,128)S(1)} %reshape.39), channel_id=1, source_target_pairs={{0,8},{8,0},{16,24},{24,16},{32,40},{40,32},{48,56},{56,48},{64,72... | collective-permute-start | bytes 73736 | tf_op jit(solution)/shard_map/ppermute | solution.py:360
